TPU v7x, 32 devices: a whole 2x2x4 slice. The times are simulated.
32 devices in a mesh: parts: 2 (over y), blk: 4 (over z), users: 2 (over x), sub: 2 (over core).
Axes of the slice: x: 2, y: 2, z: 4, core: 2. Of those that a mesh axis runs over, the one named last changes fastest.
Arguments:
- history: bfloat16 [64, 64, 256], P(('parts', 'blk'), 'users'), parts along dimension 0, may hold values from -400 to 400
- lengths: int32 [64], P(('parts', 'blk')), parts along dimension 0, may hold values from 1 to 64
- item_rows: bfloat16 [12288, 512], P(('parts', 'blk', 'users', 'sub')), parts along dimension 0, may hold values from -6 to 6
- w_query: bfloat16 [512, 256], replicated, may hold values from -0.25 to 0.25
- w_item: bfloat16 [512, 256], replicated, may hold values from -0.25 to 0.25
- w_key: bfloat16 [256, 256], replicated, may hold values from -0.375 to 0.375
- w_value: bfloat16 [256, 256], replicated, may hold values from -0.375 to 0.375
- w_pooled: bfloat16 [256, 128], replicated, may hold values from -0.25 to 0.25
- w_joint: bfloat16 [256, 128], replicated, may hold values from -0.25 to 0.25
- bias_hidden: float32 [128], replicated, may hold values from -3 to 3
- w_task: bfloat16 [128, 8], replicated, may hold values from -0.5 to 0.5
- bias_task: float32 [8], replicated, may hold values from -3 to 3
Outputs:
- logits: float32 [64, 9, 8, 1536], P(('parts', 'blk'), None, None, ('users', 'sub')), parts along dimension 0
There are 2 independent parts, one for each index of `parts`. A program takes and returns all parts, laid end to end along the dimension named above; an argument that names none is the same for every part. Nothing has to cross between parts.
All inputs are finite; a program needn't handle non-finite values.
Results may differ from a plain program's by a relative error of at most 0.011.
Values may be sent and summed in bfloat16 or wider, within the bound.
No kernel may reach another device: no remote copies, remote signals or barrier semaphores. Data moves between devices by JAX's collectives and lax.ppermute only.
A program may use at most 64 MiB of HBM per device.

v0:
```python
import math

import jax
import jax.numpy as jnp
from jax import lax
from jax.sharding import PartitionSpec as P

DH = 256
REACH = 4
WIN = 9


def shifted(block, axis, distance):
    devices = range(lax.axis_size(axis))
    route = [((i - distance) % len(devices), i) for i in devices]
    return lax.ppermute(block, axis, route)


def project(item_rows, w_query, w_item, w_joint, bias_hidden):
    queries = jnp.dot(item_rows, w_query, preferred_element_type=jnp.float32).astype(jnp.bfloat16)
    joined = jnp.dot(item_rows, w_item, preferred_element_type=jnp.float32).astype(jnp.bfloat16)
    item_terms = (
        jnp.dot(joined, w_joint, preferred_element_type=jnp.float32) + bias_hidden
    ).astype(jnp.bfloat16)
    return (queries, item_terms)


def score_pairs(queries, item_terms, key_rows, value_rows, is_valid, w_pooled, w_task, bias_task):
    scale = 1.0 / math.sqrt(queries.shape[-1])
    count_users, count_tokens, width = key_rows.shape
    flat_keys = key_rows.reshape(count_users * count_tokens, width)
    scores = jnp.einsum("id,nd->in", queries, flat_keys, preferred_element_type=jnp.float32) * scale
    scores = scores.reshape(queries.shape[0], count_users, count_tokens)
    scores = jnp.where(is_valid[None], scores, -jnp.inf)
    maximum = jnp.max(scores, axis=-1, keepdims=True)
    expo = jnp.exp(scores - maximum)
    weights = (expo / jnp.sum(expo, axis=-1, keepdims=True)).astype(jnp.bfloat16)
    pooled = jnp.einsum(
        "iut,utd->uid", weights, value_rows, preferred_element_type=jnp.float32
    ).astype(jnp.bfloat16)
    hidden = (
        jnp.einsum("uid,dh->uih", pooled, w_pooled, preferred_element_type=jnp.float32)
        + item_terms.astype(jnp.float32)[None]
    )
    hidden = jax.nn.relu(hidden).astype(jnp.bfloat16)
    logits = jnp.einsum("uih,hk->uki", hidden, w_task, preferred_element_type=jnp.float32)
    return logits + bias_task[None, :, None]


def shards(
    history,
    lengths,
    item_rows,
    w_query,
    w_item,
    w_key,
    w_value,
    w_pooled,
    w_joint,
    bias_hidden,
    w_task,
    bias_task,
):
    local = history.reshape(-1, DH)
    key_local = (
        jnp.dot(local, w_key, preferred_element_type=jnp.float32)
        .astype(jnp.bfloat16)
        .reshape(history.shape)
    )
    value_local = (
        jnp.dot(local, w_value, preferred_element_type=jnp.float32)
        .astype(jnp.bfloat16)
        .reshape(history.shape)
    )
    key_rows, value_rows = (
        lax.all_gather(key_local, "users", axis=1, tiled=True),
        lax.all_gather(value_local, "users", axis=1, tiled=True),
    )
    is_valid = jnp.arange(key_rows.shape[1], dtype=jnp.int32)[None, :] < lengths[:, None]

    def evaluate(arrived):
        queries, item_terms = project(arrived, w_query, w_item, w_joint, bias_hidden)
        return score_pairs(
            queries, item_terms, key_rows, value_rows, is_valid, w_pooled, w_task, bias_task
        )

    window = [None] * WIN
    window[REACH] = evaluate(item_rows)
    low_side = item_rows
    high_side = item_rows
    for offset in range(1, REACH + 1):
        low_side = shifted(low_side, "blk", 1)
        high_side = shifted(high_side, "blk", -1)
        window[REACH - offset] = evaluate(low_side)
        window[REACH + offset] = evaluate(high_side)
    return jnp.stack(window, axis=1)


def solution(mesh):
    placed = (
        P(("parts", "blk"), "users", None),
        P(("parts", "blk")),
        P(("parts", "blk", "users", "sub"), None),
        P(),
        P(),
        P(),
        P(),
        P(),
        P(),
        P(),
        P(),
        P(),
    )
    return jax.shard_map(
        shards,
        mesh=mesh,
        in_specs=placed,
        out_specs=P(("parts", "blk"), None, None, ("users", "sub")),
        check_vma=False,
    )
```

profile of v0, /device:TPU:0, one launch (start us, length us, event | category | flops | bytes accessed | tf_op | source)
XLA Modules:
  0.0 119.6 jit_solution(1426204656775976241)
XLA Ops:
  0.0 3.1 %collective-permute-start = (bf16[384,512]{1,0:T(8,128)(2,1)}, bf16[384,512]{1,0:T(8,128)(2,1)S(1)}, u32[]{:S(2)}, u32[]{:S(2)}) collective-permute-start(bf16[384,512]{1,0:T(8,128)(2,1)} %param.14), channel_id=1, source_target_pairs={{12,0},{0,4},{4,8},{8,12},{13,1},{1,5},{5,9},{9,13},{14,2},{2,6},{... | collective-permute-start | bytes 1179656 | tf_op jit(solution)/shard_map/ppermute | solution.py:16
  3.1 2.1 %collective-permute-start.4 = (bf16[384,512]{1,0:T(8,128)(2,1)}, bf16[384,512]{1,0:T(8,128)(2,1)S(1)}, u32[]{:S(2)}, u32[]{:S(2)}) collective-permute-start(bf16[384,512]{1,0:T(8,128)(2,1)} %param.14), channel_id=1, source_target_pairs={{4,0},{8,4},{12,8},{0,12},{5,1},{9,5},{13,9},{1,13},{6,2},{10,6},{... | collective-permute-start | bytes 1179656 | tf_op jit(solution)/shard_map/ppermute | solution.py:16
  5.2 1.2 convolution_convert_fusion.27
  6.4 5.6 %all_gather.7 = bf16[8,64,256]{2,1,0:T(8,128)(2,1)S(1)} all-gather(bf16[8,32,256]{2,1,0:T(8,128)(2,1)S(1)} %bitcast.219), channel_id=1, replica_groups=mesh['parts'=2,'blk'=4,'users'=2,'sub'=2] {'users'}, dimensions={1}, use_global_device_ids=true | all-gather | bytes 393216 | tf_op jit(solution)/shard_map/all_gather | solution.py:77
  12.0 1.2 convolution_convert_fusion.28
  13.2 5.6 %all_gather.6 = bf16[8,64,256]{2,1,0:T(8,128)(2,1)S(1)} all-gather(bf16[8,32,256]{2,1,0:T(8,128)(2,1)S(1)} %bitcast.220), channel_id=1, replica_groups=mesh['parts'=2,'blk'=4,'users'=2,'sub'=2] {'users'}, dimensions={1}, use_global_device_ids=true | all-gather | bytes 393216 | tf_op jit(solution)/shard_map/all_gather | solution.py:76
  18.9 0.6 convolution_multiply_fusion.4
  19.5 1.1 copy.18
  20.7 0.4 fusion.63
  21.1 0.7 copy-done.15
  22.1 2.3 %maximum_convert_fusion.4 = bf16[8,384,128]{2,1,0:T(8,128)(2,1)} fusion(bf16[8,64,256]{2,1,0:T(8,128)(2,1)S(1)} %all_gather.7, f32[384,128]{1,0:T(8,128)S(1)} %fusion.63, f32[384,8]{0,1:T(8,128)S(1)} %fusion.247, f32[384,8,64]{0,2,1:T(8,128)S(1)} %bitcast.216, pred[8,64]{1,0:T(8,128)(4,1)S(1)} %iota_compare_fusion, bf16[256,128]{1,0:T(8,128)(2,1)S(1)} %copy-done.19), kind=kOutput, calls=%fused_computation.22 | convolution fusion | flops 304745536 | bytes 2109952 | tf_op jit(solution)/shard_map/uid,dh->uih/dot_general | solution.py:42
  24.4 0.6 convolution_multiply_fusion.5
  25.0 1.1 copy.17
  26.1 1.4 %fusion.246 = f32[384,8]{0,1:T(8,128)S(1)} fusion(f32[384,8,64]{0,2,1:T(8,128)} %bitcast.213, pred[8,64]{1,0:T(8,128)(4,1)S(1)} %iota_compare_fusion), kind=kOutput, calls=%fused_computation.240 | output fusion | flops 589887 | bytes 799232 | tf_op jit(solution)/shard_map/sub | solution.py:36
  27.5 0.6 convolution_multiply_fusion.3
  28.1 1.2 copy.19
  29.3 0.4 fusion.65
  29.7 3.4 %maximum_convert_fusion.5 = bf16[8,384,128]{2,1,0:T(8,128)(2,1)} fusion(bf16[8,64,256]{2,1,0:T(8,128)(2,1)S(1)} %all_gather.7, f32[384,128]{1,0:T(8,128)S(1)} %fusion.65, f32[384,8]{0,1:T(8,128)S(1)} %fusion.246, f32[384,8,64]{0,2,1:T(8,128)} %bitcast.214, pred[8,64]{1,0:T(8,128)(4,1)S(1)} %iota_compare_fusion, bf16[256,128]{1,0:T(8,128)(2,1)S(1)} %copy-done.19), kind=kOutput, calls=%fused_computation.23 | convolution fusion | flops 304745536 | bytes 2109952 | tf_op jit(solution)/shard_map/uid,dh->uih/dot_general | solution.py:42
  33.2 1.1 fusion.61
  34.3 3.8 %collective-permute-start.5 = (bf16[384,512]{1,0:T(8,128)(2,1)S(1)}, bf16[384,512]{1,0:T(8,128)(2,1)S(1)}, u32[]{:S(2)}, u32[]{:S(2)}) collective-permute-start(bf16[384,512]{1,0:T(8,128)(2,1)S(1)} %collective-permute-done.4), channel_id=1, source_target_pairs={{4,0},{8,4},{12,8},{0,12},{5,1},{9,5},{13,9},{1,13},{6,2},{10,6},{... | collective-permute-start | bytes 1179656 | tf_op jit(solution)/shard_map/ppermute | solution.py:16
  38.1 0.9 fusion.248
  39.0 3.3 %maximum_convert_fusion.3 = bf16[8,384,128]{2,1,0:T(8,128)(2,1)} fusion(bf16[8,64,256]{2,1,0:T(8,128)(2,1)S(1)} %all_gather.7, f32[384,128]{1,0:T(8,128)} %fusion.61, f32[384,8]{0,1:T(8,128)} %fusion.248, f32[384,8,64]{0,2,1:T(8,128)S(1)} %bitcast.202, pred[8,64]{1,0:T(8,128)(4,1)S(1)} %iota_compare_fusion, bf16[256,128]{1,0:T(8,128)(2,1)S(1)} %copy-done.19), kind=kOutput, calls=%fused_computation.21 | convolution fusion | flops 304745536 | bytes 2109952 | tf_op jit(solution)/shard_map/uid,dh->uih/dot_general | solution.py:42
  42.2 4.7 %collective-permute-done.1 = bf16[384,512]{1,0:T(8,128)(2,1)S(1)} collective-permute-done((bf16[384,512]{1,0:T(8,128)(2,1)S(1)}, bf16[384,512]{1,0:T(8,128)(2,1)S(1)}, u32[]{:S(2)}, u32[]{:S(2)}) %collective-permute-start.1) | collective-permute-done | bytes 393248 | tf_op jit(solution)/shard_map/ppermute | solution.py:16
  47.0 0.6 convolution_multiply_fusion.6
  47.5 1.1 copy.16
  48.7 1.4 %fusion.245 = f32[384,8]{0,1:T(8,128)S(1)} fusion(f32[384,8,64]{0,2,1:T(8,128)} %bitcast.209, pred[8,64]{1,0:T(8,128)(4,1)S(1)} %iota_compare_fusion), kind=kOutput, calls=%fused_computation.239 | output fusion | flops 589887 | bytes 799232 | tf_op jit(solution)/shard_map/sub | solution.py:36
  50.1 1.5 %collective-permute-done.5 = bf16[384,512]{1,0:T(8,128)(2,1)S(1)} collective-permute-done((bf16[384,512]{1,0:T(8,128)(2,1)S(1)}, bf16[384,512]{1,0:T(8,128)(2,1)S(1)}, u32[]{:S(2)}, u32[]{:S(2)}) %collective-permute-start.5) | collective-permute-done | bytes 393248 | tf_op jit(solution)/shard_map/ppermute | solution.py:16
  51.6 0.6 convolution_multiply_fusion.2
  52.1 1.2 copy.20
  53.3 0.4 fusion.67
  53.7 3.4 %maximum_convert_fusion.6 = bf16[8,384,128]{2,1,0:T(8,128)(2,1)} fusion(bf16[8,64,256]{2,1,0:T(8,128)(2,1)S(1)} %all_gather.7, f32[384,128]{1,0:T(8,128)S(1)} %fusion.67, f32[384,8]{0,1:T(8,128)S(1)} %fusion.245, f32[384,8,64]{0,2,1:T(8,128)} %bitcast.210, pred[8,64]{1,0:T(8,128)(4,1)S(1)} %iota_compare_fusion, bf16[256,128]{1,0:T(8,128)(2,1)S(1)} %copy-done.19), kind=kOutput, calls=%fused_computation.24 | convolution fusion | flops 304745536 | bytes 2109952 | tf_op jit(solution)/shard_map/uid,dh->uih/dot_general | solution.py:42
  57.2 0.9 collective-permute-start.2
  58.1 1.1 fusion.59
  59.2 2.9 %collective-permute-start.6 = (bf16[384,512]{1,0:T(8,128)(2,1)S(1)}, bf16[384,512]{1,0:T(8,128)(2,1)S(1)}, u32[]{:S(2)}, u32[]{:S(2)}) collective-permute-start(bf16[384,512]{1,0:T(8,128)(2,1)S(1)} %collective-permute-done.5), channel_id=1, source_target_pairs={{4,0},{8,4},{12,8},{0,12},{5,1},{9,5},{13,9},{1,13},{6,2},{10,6},{... | collective-permute-start | bytes 1179656 | tf_op jit(solution)/shard_map/ppermute | solution.py:16
  62.1 0.9 fusion.249
  63.0 3.2 %maximum_convert_fusion.2 = bf16[8,384,128]{2,1,0:T(8,128)(2,1)} fusion(bf16[8,64,256]{2,1,0:T(8,128)(2,1)S(1)} %all_gather.7, f32[384,128]{1,0:T(8,128)} %fusion.59, f32[384,8]{0,1:T(8,128)} %fusion.249, f32[384,8,64]{0,2,1:T(8,128)S(1)} %bitcast.204, pred[8,64]{1,0:T(8,128)(4,1)S(1)} %iota_compare_fusion, bf16[256,128]{1,0:T(8,128)(2,1)S(1)} %copy-done.19), kind=kOutput, calls=%fused_computation.20 | convolution fusion | flops 304745536 | bytes 2109952 | tf_op jit(solution)/shard_map/uid,dh->uih/dot_general | solution.py:42
  66.2 4.8 %collective-permute-done.2 = bf16[384,512]{1,0:T(8,128)(2,1)S(1)} collective-permute-done((bf16[384,512]{1,0:T(8,128)(2,1)S(1)}, bf16[384,512]{1,0:T(8,128)(2,1)S(1)}, u32[]{:S(2)}, u32[]{:S(2)}) %collective-permute-start.2) | collective-permute-done | bytes 393248 | tf_op jit(solution)/shard_map/ppermute | solution.py:16
  71.0 0.6 convolution_multiply_fusion.7
  71.6 1.1 copy.15
  72.7 1.4 %fusion.244 = f32[384,8]{0,1:T(8,128)S(1)} fusion(f32[384,8,64]{0,2,1:T(8,128)} %bitcast.211, pred[8,64]{1,0:T(8,128)(4,1)S(1)} %iota_compare_fusion), kind=kOutput, calls=%fused_computation.238 | output fusion | flops 589887 | bytes 799232 | tf_op jit(solution)/shard_map/sub | solution.py:36
  74.1 3.6 %collective-permute-done.6 = bf16[384,512]{1,0:T(8,128)(2,1)S(1)} collective-permute-done((bf16[384,512]{1,0:T(8,128)(2,1)S(1)}, bf16[384,512]{1,0:T(8,128)(2,1)S(1)}, u32[]{:S(2)}, u32[]{:S(2)}) %collective-permute-start.6) | collective-permute-done | bytes 393248 | tf_op jit(solution)/shard_map/ppermute | solution.py:16
  77.8 0.6 convolution_multiply_fusion.1
  78.3 1.1 copy.21
  79.9 3.5 %maximum_convert_fusion.7 = bf16[8,384,128]{2,1,0:T(8,128)(2,1)} fusion(bf16[8,64,256]{2,1,0:T(8,128)(2,1)S(1)} %all_gather.7, f32[384,128]{1,0:T(8,128)S(1)} %fusion.69, f32[384,8]{0,1:T(8,128)S(1)} %fusion.244, f32[384,8,64]{0,2,1:T(8,128)} %bitcast.212, pred[8,64]{1,0:T(8,128)(4,1)S(1)} %iota_compare_fusion, bf16[256,128]{1,0:T(8,128)(2,1)S(1)} %copy-done.19), kind=kOutput, calls=%fused_computation.25 | convolution fusion | flops 304745536 | bytes 2109952 | tf_op jit(solution)/shard_map/uid,dh->uih/dot_general | solution.py:42
  83.4 0.5 collective-permute-start.3
  83.9 1.1 fusion.57
  85.1 3.3 %collective-permute-start.7 = (bf16[384,512]{1,0:T(8,128)(2,1)S(1)}, bf16[384,512]{1,0:T(8,128)(2,1)S(1)}, u32[]{:S(2)}, u32[]{:S(2)}) collective-permute-start(bf16[384,512]{1,0:T(8,128)(2,1)S(1)} %collective-permute-done.6), channel_id=1, source_target_pairs={{4,0},{8,4},{12,8},{0,12},{5,1},{9,5},{13,9},{1,13},{6,2},{10,6},{... | collective-permute-start | bytes 1179656 | tf_op jit(solution)/shard_map/ppermute | solution.py:16
  88.3 0.9 fusion.250
  89.2 3.2 %maximum_convert_fusion.1 = bf16[8,384,128]{2,1,0:T(8,128)(2,1)} fusion(bf16[8,64,256]{2,1,0:T(8,128)(2,1)S(1)} %all_gather.7, f32[384,128]{1,0:T(8,128)} %fusion.57, f32[384,8]{0,1:T(8,128)} %fusion.250, f32[384,8,64]{0,2,1:T(8,128)S(1)} %bitcast.206, pred[8,64]{1,0:T(8,128)(4,1)S(1)} %iota_compare_fusion, bf16[256,128]{1,0:T(8,128)(2,1)S(1)} %copy-done.19), kind=kOutput, calls=%fused_computation.19 | convolution fusion | flops 304745536 | bytes 2109952 | tf_op jit(solution)/shard_map/uid,dh->uih/dot_general | solution.py:42
  92.5 4.8 %collective-permute-done.3 = bf16[384,512]{1,0:T(8,128)(2,1)S(1)} collective-permute-done((bf16[384,512]{1,0:T(8,128)(2,1)S(1)}, bf16[384,512]{1,0:T(8,128)(2,1)S(1)}, u32[]{:S(2)}, u32[]{:S(2)}) %collective-permute-start.3) | collective-permute-done | bytes 393248 | tf_op jit(solution)/shard_map/ppermute | solution.py:16
  97.2 0.6 convolution_multiply_fusion.8
  97.8 1.1 copy.14
  99.0 2.0 %fusion.243 = f32[384,8]{0,1:T(8,128)} fusion(f32[384,8,64]{0,2,1:T(8,128)} %bitcast.207, pred[8,64]{1,0:T(8,128)(4,1)S(1)} %iota_compare_fusion), kind=kOutput, calls=%fused_computation.237 | output fusion | flops 589887 | bytes 799232 | tf_op jit(solution)/shard_map/sub | solution.py:36
  101.0 3.2 %collective-permute-done.7 = bf16[384,512]{1,0:T(8,128)(2,1)S(1)} collective-permute-done((bf16[384,512]{1,0:T(8,128)(2,1)S(1)}, bf16[384,512]{1,0:T(8,128)(2,1)S(1)}, u32[]{:S(2)}, u32[]{:S(2)}) %collective-permute-start.7) | collective-permute-done | bytes 393248 | tf_op jit(solution)/shard_map/ppermute | solution.py:16
  104.2 0.6 convolution_multiply_fusion
  105.1 0.9 fusion.251
  106.5 3.5 %maximum_convert_fusion.8 = bf16[8,384,128]{2,1,0:T(8,128)(2,1)} fusion(bf16[8,64,256]{2,1,0:T(8,128)(2,1)S(1)} %all_gather.7, f32[384,128]{1,0:T(8,128)S(1)} %fusion.71, f32[384,8]{0,1:T(8,128)S(1)} %copy-done.22, f32[384,8,64]{0,2,1:T(8,128)} %bitcast.208, pred[8,64]{1,0:T(8,128)(4,1)S(1)} %iota_compare_fusion, bf16[256,128]{1,0:T(8,128)(2,1)S(1)} %copy-done.19), kind=kOutput, calls=%fused_computation.26 | convolution fusion | flops 304745536 | bytes 2109952 | tf_op jit(solution)/shard_map/uid,dh->uih/dot_general | solution.py:42
  110.0 1.5 %fusion.89 = f32[8,9,8,384]{3,2,0,1:T(8,128)S(1)} fusion(bf16[8,384,128]{2,1,0:T(8,128)(2,1)} %maximum_convert_fusion.8, f32[8]{0:T(128)S(1)} %copy-done.18, bf16[128,8]{0,1:T(8,128)(2,1)S(1)} %copy-done.16), kind=kOutput, calls=%fused_computation.145 | convolution fusion | flops 6316031 | bytes 886816 | tf_op jit(solution)/shard_map/uih,hk->uki/dot_general | solution.py:46
  112.2 0.5 copy-done.5
  113.3 0.5 copy-done.6
  114.5 0.5 copy-done.9
  115.3 0.4 fusion.55
  115.8 2.5 %maximum_convert_fusion = bf16[8,384,128]{2,1,0:T(8,128)(2,1)S(1)} fusion(bf16[8,64,256]{2,1,0:T(8,128)(2,1)S(1)} %all_gather.7, f32[384,128]{1,0:T(8,128)S(1)} %fusion.55, f32[384,8]{0,1:T(8,128)S(1)} %copy-done.21, f32[384,8,64]{0,2,1:T(8,128)} %bitcast.200, pred[8,64]{1,0:T(8,128)(4,1)S(1)} %iota_compare_fusion, bf16[256,128]{1,0:T(8,128)(2,1)S(1)} %copy-done.19), kind=kOutput, calls=%fused_computation.18 | convolution fusion | flops 304745536 | bytes 2109952 | tf_op jit(solution)/shard_map/uid,dh->uih/dot_general | solution.py:42
  118.7 1.0 copy.23
  (58 shorter events, 4.2 us)
Async XLA Ops:
  0.0 18.9 %copy-start = (bf16[512,256]{1,0:T(8,128)(2,1)S(1)}, bf16[512,256]{1,0:T(8,128)(2,1)}, u32[]{:S(2)}) copy-start(bf16[512,256]{1,0:T(8,128)(2,1)} %param.15) | copy-start | bytes 786436
  0.0 18.9 %copy-start.3 = (bf16[384,512]{1,0:T(8,128)(2,1)S(1)}, bf16[384,512]{1,0:T(8,128)(2,1)}, u32[]{:S(2)}) copy-start(bf16[384,512]{1,0:T(8,128)(2,1)} %param.14) | copy-start | bytes 1179652
  0.0 18.8 %copy-start.20 = (s32[8]{0:T(128)S(1)}, s32[8]{0:T(128)}, u32[]{:S(2)}) copy-start(s32[8]{0:T(128)} %param.13) | copy-start | bytes 100
  0.0 24.4 %collective-permute-start = (bf16[384,512]{1,0:T(8,128)(2,1)}, bf16[384,512]{1,0:T(8,128)(2,1)S(1)}, u32[]{:S(2)}, u32[]{:S(2)}) collective-permute-start(bf16[384,512]{1,0:T(8,128)(2,1)} %param.14), channel_id=1, source_target_pairs={{12,0},{0,4},{4,8},{8,12},{13,1},{1,5},{5,9},{9,13},{14,2},{2,6},{... | collective-permute-start | bytes 1179656 | tf_op jit(solution)/shard_map/ppermute | solution.py:16
  3.1 24.4 %collective-permute-start.4 = (bf16[384,512]{1,0:T(8,128)(2,1)}, bf16[384,512]{1,0:T(8,128)(2,1)S(1)}, u32[]{:S(2)}, u32[]{:S(2)}) collective-permute-start(bf16[384,512]{1,0:T(8,128)(2,1)} %param.14), channel_id=1, source_target_pairs={{4,0},{8,4},{12,8},{0,12},{5,1},{9,5},{13,9},{1,13},{6,2},{10,6},{... | collective-permute-start | bytes 1179656 | tf_op jit(solution)/shard_map/ppermute | solution.py:16
  19.5 1.2 copy-start.1
  19.5 1.2 copy-start.2
  19.5 1.2 copy-start.17
  20.7 1.1 copy-start.15
  20.7 1.4 %copy-start.19 = (bf16[256,128]{1,0:T(8,128)(2,1)S(1)}, bf16[256,128]{1,0:T(8,128)(2,1)}, u32[]{:S(2)}) copy-start(bf16[256,128]{1,0:T(8,128)(2,1)} %param.19) | copy-start | bytes 196612
  33.2 4.9 %copy-start.12 = (f32[384,512]{0,1:T(8,128)S(1)}, f32[384,512]{0,1:T(8,128)}, u32[]{:S(2)}) copy-start(f32[384,512]{0,1:T(8,128)} %copy.19) | copy-start | bytes 2359300
  33.2 13.8 %collective-permute-start.1 = (bf16[384,512]{1,0:T(8,128)(2,1)S(1)}, bf16[384,512]{1,0:T(8,128)(2,1)S(1)}, u32[]{:S(2)}, u32[]{:S(2)}) collective-permute-start(bf16[384,512]{1,0:T(8,128)(2,1)S(1)} %collective-permute-done), channel_id=1, source_target_pairs={{12,0},{0,4},{4,8},{8,12},{13,1},{1,5},{5,9},{9,13},{14,2},{2,6},{... | collective-permute-start | bytes 1179656 | tf_op jit(solution)/shard_map/ppermute | solution.py:16
  34.3 17.3 %collective-permute-start.5 = (bf16[384,512]{1,0:T(8,128)(2,1)S(1)}, bf16[384,512]{1,0:T(8,128)(2,1)S(1)}, u32[]{:S(2)}, u32[]{:S(2)}) collective-permute-start(bf16[384,512]{1,0:T(8,128)(2,1)S(1)} %collective-permute-done.4), channel_id=1, source_target_pairs={{4,0},{8,4},{12,8},{0,12},{5,1},{9,5},{13,9},{1,13},{6,2},{10,6},{... | collective-permute-start | bytes 1179656 | tf_op jit(solution)/shard_map/ppermute | solution.py:16
  57.2 4.9 %copy-start.13 = (f32[384,512]{0,1:T(8,128)S(1)}, f32[384,512]{0,1:T(8,128)}, u32[]{:S(2)}) copy-start(f32[384,512]{0,1:T(8,128)} %copy.20) | copy-start | bytes 2359300
  57.2 13.8 %collective-permute-start.2 = (bf16[384,512]{1,0:T(8,128)(2,1)S(1)}, bf16[384,512]{1,0:T(8,128)(2,1)S(1)}, u32[]{:S(2)}, u32[]{:S(2)}) collective-permute-start(bf16[384,512]{1,0:T(8,128)(2,1)S(1)} %collective-permute-done.1), channel_id=1, source_target_pairs={{12,0},{0,4},{4,8},{8,12},{13,1},{1,5},{5,9},{9,13},{14,2},{2,6},{... | collective-permute-start | bytes 1179656 | tf_op jit(solution)/shard_map/ppermute | solution.py:16
  59.2 18.6 %collective-permute-start.6 = (bf16[384,512]{1,0:T(8,128)(2,1)S(1)}, bf16[384,512]{1,0:T(8,128)(2,1)S(1)}, u32[]{:S(2)}, u32[]{:S(2)}) collective-permute-start(bf16[384,512]{1,0:T(8,128)(2,1)S(1)} %collective-permute-done.5), channel_id=1, source_target_pairs={{4,0},{8,4},{12,8},{0,12},{5,1},{9,5},{13,9},{1,13},{6,2},{10,6},{... | collective-permute-start | bytes 1179656 | tf_op jit(solution)/shard_map/ppermute | solution.py:16
  83.4 4.9 %copy-start.14 = (f32[384,512]{0,1:T(8,128)S(1)}, f32[384,512]{0,1:T(8,128)}, u32[]{:S(2)}) copy-start(f32[384,512]{0,1:T(8,128)} %copy.21) | copy-start | bytes 2359300
  83.4 13.8 %collective-permute-start.3 = (bf16[384,512]{1,0:T(8,128)(2,1)S(1)}, bf16[384,512]{1,0:T(8,128)(2,1)S(1)}, u32[]{:S(2)}, u32[]{:S(2)}) collective-permute-start(bf16[384,512]{1,0:T(8,128)(2,1)S(1)} %collective-permute-done.2), channel_id=1, source_target_pairs={{12,0},{0,4},{4,8},{8,12},{13,1},{1,5},{5,9},{9,13},{14,2},{2,6},{... | collective-permute-start | bytes 1179656 | tf_op jit(solution)/shard_map/ppermute | solution.py:16
  85.1 19.2 %collective-permute-start.7 = (bf16[384,512]{1,0:T(8,128)(2,1)S(1)}, bf16[384,512]{1,0:T(8,128)(2,1)S(1)}, u32[]{:S(2)}, u32[]{:S(2)}) collective-permute-start(bf16[384,512]{1,0:T(8,128)(2,1)S(1)} %collective-permute-done.6), channel_id=1, source_target_pairs={{4,0},{8,4},{12,8},{0,12},{5,1},{9,5},{13,9},{1,13},{6,2},{10,6},{... | collective-permute-start | bytes 1179656 | tf_op jit(solution)/shard_map/ppermute | solution.py:16
  105.1 1.3 %copy-start.11 = (f32[384,512]{0,1:T(8,128)}, f32[384,512]{0,1:T(8,128)S(1)}, u32[]{:S(2)}) copy-start(f32[384,512]{0,1:T(8,128)S(1)} %copy.22) | copy-start | bytes 2359300
  105.1 1.3 %copy-start.22 = (f32[384,8]{0,1:T(8,128)S(1)}, f32[384,8]{0,1:T(8,128)}, u32[]{:S(2)}) copy-start(f32[384,8]{0,1:T(8,128)} %fusion.243) | copy-start | bytes 36868
  106.4 3.5 %copy-start.16 = (bf16[128,8]{0,1:T(8,128)(2,1)S(1)}, bf16[128,8]{0,1:T(8,128)(2,1)}, u32[]{:S(2)}) copy-start(bf16[128,8]{0,1:T(8,128)(2,1)} %param.22) | copy-start | bytes 6148
  106.5 3.5 %copy-start.18 = (f32[8]{0:T(128)S(1)}, f32[8]{0:T(128)}, u32[]{:S(2)}) copy-start(f32[8]{0:T(128)} %param.23) | copy-start | bytes 100
  106.5 5.0 %copy-start.10 = (bf16[8,384,128]{2,1,0:T(8,128)(2,1)S(1)}, bf16[8,384,128]{2,1,0:T(8,128)(2,1)}, u32[]{:S(2)}) copy-start(bf16[8,384,128]{2,1,0:T(8,128)(2,1)} %maximum_convert_fusion.7) | copy-start | bytes 2359300
  110.0 1.8 %copy-start.7 = (bf16[8,384,128]{2,1,0:T(8,128)(2,1)S(1)}, bf16[8,384,128]{2,1,0:T(8,128)(2,1)}, u32[]{:S(2)}) copy-start(bf16[8,384,128]{2,1,0:T(8,128)(2,1)} %maximum_convert_fusion.6) | copy-start | bytes 2359300
  111.5 1.2 copy-start.5
  111.8 1.2 %copy-start.4 = (bf16[8,384,128]{2,1,0:T(8,128)(2,1)S(1)}, bf16[8,384,128]{2,1,0:T(8,128)(2,1)}, u32[]{:S(2)}) copy-start(bf16[8,384,128]{2,1,0:T(8,128)(2,1)} %maximum_convert_fusion.4) | copy-start | bytes 2359300
  112.7 1.2 copy-start.6
  113.0 1.2 copy-start.8
  113.8 1.2 copy-start.9
  115.0 0.8 copy-start.21
where the time goes:
time: 120 us
  matrix products  45.7 us (38%)
  waiting for transfers between devices  22.6 us (19%)
  starting transfers between devices  16.7 us (14%)
  local copies, waits for them, and re-layouts  12.9 us (11%)
  blocking collectives  11.3 us (9%)
  other arithmetic  10.2 us (8%)
    dot_general x9, matrix products, score_pairs(): jnp.einsum('uid,dh->uih', pooled, w_pooled, preferred_element_type=jnp.fl...  28.4 us
    ppermute x8, waiting for transfers between devices, shifted(): return lax.ppermute(block, axis, route)  22.6 us
    ppermute x8, starting transfers between devices, shifted(): return lax.ppermute(block, axis, route)  16.7 us
    sub x9, other arithmetic, score_pairs(): expo = jnp.exp(scores - maximum)  10.1 us
    mul x9, local copies, waits for them, and re-layouts, score_pairs(): jnp.einsum('id,nd->in', queries, flat_keys, preferred_element_type=jnp.fl...  9.49 us
    dot_general x9, matrix products, project(): jnp.dot(joined, w_joint, preferred_element_type=jnp.float32) + bias_hidden  5.93 us
    all_gather x1, blocking collectives, shards(): lax.all_gather(value_local, 'users', axis=1, tiled=True)  5.64 us
    all_gather x1, blocking collectives, shards(): lax.all_gather(key_local, 'users', axis=1, tiled=True)  5.64 us
  transfers between devices with their start and end apart: 8, of which 6 were waited for; matrix products, arithmetic and copies ran while one was open for 30% of the time, Pallas kernels for 0%

commit v1 on v0

v1 whole, which is shorter than its diff:
```python
import functools
import math

import jax
import jax.numpy as jnp
from jax import lax
from jax.experimental import pallas as pl
from jax.experimental.pallas import tpu as pltpu
from jax.sharding import PartitionSpec as P

REACH = 4
WIN = 2 * REACH + 1
LENGTH_ROWS = 16
BF16 = jnp.bfloat16
F32 = jnp.float32
VMEM = pl.BlockSpec(memory_space=pltpu.VMEM)
SMEM = pl.BlockSpec(memory_space=pltpu.SMEM)
ANY = pl.BlockSpec(memory_space=pl.ANY)


def call(kernel, out_shape, in_specs, out_specs, args, flops, scratch=()):
    moved = sum(math.prod(a.shape) * a.dtype.itemsize for a in args)
    return pl.pallas_call(
        kernel,
        out_shape=out_shape,
        in_specs=in_specs,
        out_specs=out_specs,
        scratch_shapes=list(scratch),
        cost_estimate=pl.CostEstimate(flops=flops, bytes_accessed=moved, transcendentals=0),
    )(*args)


def pack_kernel(lengths_ref, history_ref, piece_ref):
    rows, width = piece_ref.shape
    tokens = history_ref.shape[1]
    users = (rows - LENGTH_ROWS) // tokens
    first = lax.axis_index("sub") * users
    piece_ref[: users * tokens, :] = history_ref[pl.ds(first, users)].reshape(users * tokens, width)
    row = lax.broadcasted_iota(jnp.int32, (LENGTH_ROWS, width), 0)
    lengths = jnp.zeros((LENGTH_ROWS, width), F32)
    for user in range(users):
        lengths = jnp.where(row == user, lengths_ref[first + user].astype(F32), lengths)
    piece_ref[users * tokens :, :] = lengths.astype(BF16)


def project_kernel(items_ref, w_query_ref, w_item_ref, w_joint_ref, bias_ref, out_ref):
    width = w_query_ref.shape[1]
    rows = items_ref[...]
    queries = jnp.dot(rows, w_query_ref[...], preferred_element_type=F32)
    out_ref[:width, :] = queries.T.astype(BF16)
    joined = jnp.dot(rows, w_item_ref[...], preferred_element_type=F32).astype(BF16)
    terms = jnp.dot(joined, w_joint_ref[...], preferred_element_type=F32) + bias_ref[...]
    out_ref[width:, :] = terms.T.astype(BF16)


def keys_values(pieces, w_key_ref, w_value_ref, w_pooled_ref, key_ref, pooled_ref, mask_ref, turn):
    users, count, width = key_ref.shape
    share = users // len(pieces)
    w_pooled = w_pooled_ref[...].astype(F32).T.astype(BF16)
    for s, parts in enumerate(pieces):
        tokens = count // len(parts)
        lengths = turn[s]
        for r, (rows, first) in enumerate(parts):
            keys = jnp.dot(rows, w_key_ref[...], preferred_element_type=F32).astype(BF16)
            values = jnp.dot(rows, w_value_ref[...], preferred_element_type=F32).astype(BF16)
            place = slice(r * tokens, (r + 1) * tokens)
            at = lax.broadcasted_iota(jnp.int32, (tokens, 128), 0) + first
            at = at.astype(F32)
            for u in range(share):
                user = s * share + u
                key_ref[user, place, :] = keys[u * tokens : (u + 1) * tokens]
                pooled = lax.dot_general(
                    w_pooled,
                    values[u * tokens : (u + 1) * tokens],
                    (((1,), (1,)), ((), ())),
                    preferred_element_type=F32,
                )
                pooled_ref[user, :, place] = pooled.astype(BF16)
                mask_ref[user, place, :] = jnp.where(at < lengths[u : u + 1, :128], 0.0, -jnp.inf)


def score(items_ref, key_ref, pooled_ref, mask_ref, w_task_ref, bias_task_ref, out_ref, shares):
    users, _, width = key_ref.shape
    tasks = w_task_ref.shape[1]
    hid = w_task_ref.shape[0]
    share = users // shares
    factor = math.log2(math.e) / math.sqrt(width)
    queries = items_ref[:width, :]
    terms = items_ref[width:, :].astype(F32)
    columns = terms.shape[1]
    w_task = w_task_ref[...].astype(F32).T
    blank = jnp.zeros_like(w_task)
    heads = jnp.concatenate(
        [jnp.concatenate([w_task, blank], 1), jnp.concatenate([blank, w_task], 1)], 0
    ).astype(BF16)
    row = lax.broadcasted_iota(jnp.int32, (2 * tasks, columns), 0)
    bias = jnp.zeros((2 * tasks, columns), F32)
    for task in range(tasks):
        bias = jnp.where(row % tasks == task, bias_task_ref[task], bias)

    def hidden(user):
        scores = jnp.dot(key_ref[user], queries, preferred_element_type=F32)
        mask = mask_ref[user]
        scores = scores + jnp.concatenate([mask] * (columns // 128), 1)
        maximum = jnp.max(scores, axis=0, keepdims=True)
        expo = jnp.exp2((scores - maximum) * factor)
        weights = (expo * (1.0 / jnp.sum(expo, axis=0, keepdims=True))).astype(BF16)
        total = jnp.dot(pooled_ref[user], weights, preferred_element_type=F32) + terms
        return jnp.maximum(total, 0.0).astype(BF16)

    for s in range(shares):
        first = lax.rem(lax.axis_index("sub") + s, shares) * share
        for u in range(0, share, 2):
            both = jnp.concatenate([hidden(s * share + u), hidden(s * share + u + 1)], 0)
            logits = jnp.dot(heads, both, preferred_element_type=F32) + bias
            if len(out_ref.shape) == 3:
                out_ref[first + u] = logits[:tasks]
                out_ref[first + u + 1] = logits[tasks:]
            else:
                place = pl.multiple_of((first + u) * tasks, 2 * tasks)
                out_ref[pl.ds(place, 2 * tasks), :] = logits.astype(out_ref.dtype)


def first_kernel(own, shares, parts, *refs):
    if own:
        history_ref, refs = refs[0], refs[1:]
    given = [own and s > 0 and r == 0 and parts > 1 for s in range(shares) for r in range(parts)]
    count = given.count(False)
    sent, refs = list(refs[:count]), refs[count:]
    piece_refs = [None if local else sent.pop(0) for local in given]
    w_key_ref, w_value_ref, w_pooled_ref, items_ref, w_task_ref, bias_task_ref = refs[:6]
    out_ref, key_ref, pooled_ref, mask_ref = refs[6:]
    me, side = lax.axis_index("users"), lax.axis_index("sub")
    pieces, turn = [], []
    rows = piece_refs[0].shape[0] - LENGTH_ROWS
    for s in range(shares):
        entries = []
        for r in range(parts):
            ref = piece_refs[s * parts + r]
            if own and s > 0 and r == 0:
                users = history_ref.shape[0] // shares
                chosen = history_ref[pl.ds(lax.rem(side + s, shares) * users, users)]
                content = chosen.reshape(rows, history_ref.shape[2])
            else:
                content = ref[:rows, :]
            tokens = key_ref.shape[1] // parts
            entries.append((content, lax.rem(me + r, parts) * tokens))
        pieces.append(entries)
        turn.append(piece_refs[s * parts + parts - 1][rows:, :].astype(F32))
    keys_values(pieces, w_key_ref, w_value_ref, w_pooled_ref, key_ref, pooled_ref, mask_ref, turn)
    score(items_ref, key_ref, pooled_ref, mask_ref, w_task_ref, bias_task_ref, out_ref, shares)


def next_kernel(shares, items_ref, key_ref, pooled_ref, mask_ref, w_task_ref, bias_task_ref, out_ref):
    score(items_ref, key_ref, pooled_ref, mask_ref, w_task_ref, bias_task_ref, out_ref, shares)


def place_kernel(count, *refs):
    own_refs, away_refs, (out_ref, held, sems) = refs[:2], refs[2:count], refs[count:]
    users, _, tasks, _ = out_ref.shape
    me = lax.axis_index("blk")
    copies = []
    for at, ref in enumerate(own_refs):
        held[at] = ref[...]
    for at, ref in enumerate(away_refs):
        for user in range(0, users, 2):
            both = ref[user * tasks : (user + 2) * tasks, :].astype(F32)
            held[at + 2, user] = both[:tasks]
            held[at + 2, user + 1] = both[tasks:]
    for position in range(WIN):
        block = lax.rem(me + (position - REACH) % count, count)
        ahead = lax.rem(block // 2 - me // 2 + count // 2, count // 2)
        source = 2 * ahead + lax.rem(block + me, 2)
        copy = pltpu.make_async_copy(held.at[source], out_ref.at[:, position], sems.at[position])
        copy.start()
        copies.append(copy)
    for copy in copies:
        copy.wait()


def shift(block, axis, distance):
    count = lax.axis_size(axis)
    return lax.ppermute(block, axis, [((i + distance) % count, i) for i in range(count)])


def from_pair(block, distance):
    count = lax.axis_size("blk")
    return lax.ppermute(block, "blk", [((i + 2 * distance) % count, i) for i in range(count)])


def spread(piece, shares, parts, own=False):
    row = [piece] + [shift(piece, "users", r) for r in range(1, parts)]
    table = [row]
    for s in range(1, shares):
        away = [shift(entry, "sub", s) for entry in row[1:]]
        table.append([None if own and parts > 1 else shift(piece, "sub", s)] + away)
    return table


def shards(
    history,
    lengths,
    item_rows,
    w_query,
    w_item,
    w_key,
    w_value,
    w_pooled,
    w_joint,
    bias_hidden,
    w_task,
    bias_task,
):
    users, tokens, width = history.shape
    items = item_rows.shape[0]
    hid, tasks = w_task.shape
    count, parts, shares = (lax.axis_size(axis) for axis in ("blk", "users", "sub"))
    full = tokens * parts

    piece = call(
        pack_kernel,
        jax.ShapeDtypeStruct((users // shares * tokens + LENGTH_ROWS, width), BF16),
        [SMEM, VMEM],
        VMEM,
        (lengths, history),
        0,
    )
    mine = call(
        project_kernel,
        jax.ShapeDtypeStruct((width + hid, items), BF16),
        [VMEM] * 5,
        VMEM,
        (item_rows, w_query, w_item, w_joint, bias_hidden[None]),
        2 * items * item_rows.shape[1] * 2 * width,
    )
    flops = 2 * users * items * (full * (width + hid) + hid * tasks)
    state = (
        jax.ShapeDtypeStruct((users, full, width), BF16),
        jax.ShapeDtypeStruct((users, hid, full), BF16),
        jax.ShapeDtypeStruct((users, full, 128), F32),
    )
    kept = jax.ShapeDtypeStruct((users, tasks, items), F32)
    sent = jax.ShapeDtypeStruct((users * tasks, items), BF16)

    def start(table, block, out, own):
        flat = [entry for row in table for entry in row if entry is not None]
        head = [history] if own else []
        result = call(
            functools.partial(first_kernel, own, shares, parts),
            (out, *state),
            [VMEM] * (len(head) + len(flat) + 5) + [SMEM],
            [VMEM] * 4,
            (*head, *flat, w_key, w_value, w_pooled, block, w_task, bias_task),
            flops + 4 * users * full * width * width,
        )
        return result[0], result[1:]

    def go_on(held, block, out):
        return call(
            functools.partial(next_kernel, shares),
            out,
            [VMEM] * 5 + [SMEM],
            VMEM,
            (block, *held, w_task, bias_task),
            flops,
        )

    if count % 2 or count > WIN:
        window = [None] * WIN
        window[REACH], held = start(spread(piece, shares, parts, True), mine, kept, True)
        low = high = mine
        for offset in range(1, REACH + 1):
            low, high = shift(low, "blk", -1), shift(high, "blk", 1)
            window[REACH - offset] = go_on(held, low, kept)
            window[REACH + offset] = go_on(held, high, kept)
        return jnp.stack(window, axis=1)

    far = [from_pair(piece, ahead) for ahead in range(1, count // 2)]
    own = spread(piece, shares, parts, True)
    other = lax.ppermute(mine, "blk", [(i ^ 1, i) for i in range(count)])
    at_home, held = start(own, mine, kept, True)
    away = []
    for ahead, entry in enumerate(far, 1):
        near, guests = start(spread(entry, shares, parts), mine, sent, False)
        back = [from_pair(near, -ahead)]
        back.append(from_pair(go_on(guests, other, sent), -ahead))
        away.append(back)
    beside = go_on(held, other, kept)
    results = [entry for back in reversed(away) for entry in back]
    return call(
        functools.partial(place_kernel, count),
        jax.ShapeDtypeStruct((users, WIN, tasks, items), F32),
        [VMEM] * count,
        ANY,
        (at_home, beside, *results),
        0,
        (pltpu.VMEM((count, users, tasks, items), F32), pltpu.SemaphoreType.DMA((WIN,))),
    )


def solution(mesh):
    placed = (
        P(("parts", "blk"), "users", None),
        P(("parts", "blk")),
        P(("parts", "blk", "users", "sub"), None),
        P(),
        P(),
        P(),
        P(),
        P(),
        P(),
        P(),
        P(),
        P(),
    )
    return jax.shard_map(
        shards,
        mesh=mesh,
        in_specs=placed,
        out_specs=P(("parts", "blk"), None, None, ("users", "sub")),
        check_vma=False,
    )
```

time: 120 us -> 48.3 us (0.40)
  matrix products: 45.7 us -> 0 us
  Pallas kernels: 0 us -> 24.9 us
  waiting for transfers between devices: 22.6 us -> 8.05 us
  blocking collectives: 11.3 us -> 0 us
  other arithmetic: 10.2 us -> 0 us
  local copies, waits for them, and re-layouts: 12.9 us -> 3.89 us
  starting transfers between devices: 16.7 us -> 11 us
    dot_general x38 -> x0, matrix products: 45.7 us -> none  [the longest x9 28.4 us: score_pairs(): jnp.einsum('uid,dh->uih', pooled, w_pooled, preferred_element_type=jnp.fl...]
    pallas_call x0 -> x7, Pallas kernels: none -> 24.9 us  [call(): pl.pallas_call(kernel, out_shape=out_shape, in_specs=in_specs, out_specs=...]
    ppermute x8 -> x9, waiting for transfers between devices: 22.6 us -> 8.05 us  [the longest x5 4.03 us: shift(): lax.ppermute(block, axis, [((i + distance) % count, i) for i in range(cou...]
    all_gather x2 -> x0, blocking collectives: 11.3 us -> none  [the longest x1 5.64 us: shards(): lax.all_gather(value_local, 'users', axis=1, tiled=True)]
    sub x9 -> x0, other arithmetic: 10.1 us -> none  [score_pairs(): expo = jnp.exp(scores - maximum)]
    mul x9 -> x0, local copies, waits for them, and re-layouts: 9.49 us -> none  [score_pairs(): jnp.einsum('id,nd->in', queries, flat_keys, preferred_element_type=jnp.fl...]
    ppermute x8 -> x9, starting transfers between devices: 16.7 us -> 11 us  [the longest x3 5.96 us: from_pair(): lax.ppermute(block, 'blk', [((i + 2 * distance) % count, i) for i in rang...]
    unnamed x46 -> x21, local copies, waits for them, and re-layouts: 2.44 us -> 3.89 us
  transfers between devices with their start and end apart: 8 -> 9, of which waited for: 6 -> 3; matrix products, arithmetic and copies ran while one was open for 30% -> 1% of each run, Pallas kernels for 0% -> 43%
where the time goes in v1:
time: 48.3 us; the launch traced here: 47.9 us
  Pallas kernels  24.9 us (52%)
  starting transfers between devices  11 us (23%)
  waiting for transfers between devices  8.05 us (17%)
  local copies, waits for them, and re-layouts  3.89 us (8%)
    pallas_call x7, Pallas kernels, call(): pl.pallas_call(kernel, out_shape=out_shape, in_specs=in_specs, out_specs=...  24.9 us
    ppermute x3, starting transfers between devices, from_pair(): lax.ppermute(block, 'blk', [((i + 2 * distance) % count, i) for i in rang...  5.96 us
    ppermute x5, waiting for transfers between devices, shift(): lax.ppermute(block, axis, [((i + distance) % count, i) for i in range(cou...  4.03 us
    ppermute x3, waiting for transfers between devices, from_pair(): lax.ppermute(block, 'blk', [((i + 2 * distance) % count, i) for i in rang...  4.02 us
    unnamed x21, local copies, waits for them, and re-layouts  3.89 us
    ppermute x1, starting transfers between devices, shards(): other = lax.ppermute(mine, 'blk', [(i ^ 1, i) for i in range(count)])  3.06 us
    ppermute x5, starting transfers between devices, shift(): lax.ppermute(block, axis, [((i + distance) % count, i) for i in range(cou...  2.03 us
  transfers between devices with their start and end apart: 9, of which 3 were waited for; matrix products, arithmetic and copies ran while one was open for 1% of the time, Pallas kernels for 43%

profile of v1, /device:TPU:0, one launch (start us, length us, event | category | flops | bytes accessed | tf_op | source)
XLA Modules:
  0.0 47.9 jit_solution(1459874355383369418)
XLA Ops:
  0.0 2.5 %shard_map.119.refs_7_ = bf16[384,384]{1,0:T(8,128)(2,1)} custom-call(bf16[384,512]{1,0:T(8,128)(2,1)} %items_ref.1, bf16[512,256]{1,0:T(8,128)(2,1)} %w_query_ref.1, bf16[512,256]{1,0:T(8,128)(2,1)} %w_item_ref.1, bf16[256,128]{1,0:T(8,128)(2,1)} %w_joint_ref.1, f32[1,128]{1,0:T(1,128)} %bitcast.1), custom_call_target="tpu_custom_call" | custom-call | flops 201326592 | bytes 983552 | tf_op jit(solution)/shard_map/pallas_call | solution.py:23
  2.5 0.0 copy-start.3
  2.5 3.1 %collective-permute-start.2 = (bf16[384,384]{1,0:T(8,128)(2,1)}, bf16[384,384]{1,0:T(8,128)(2,1)S(1)}, u32[]{:S(2)}, u32[]{:S(2)}) collective-permute-start(bf16[384,384]{1,0:T(8,128)(2,1)} %shard_map.119.refs_7_), channel_id=1, source_target_pairs={{4,0},{0,4},{12,8},{8,12},{5,1},{1,5},{13,9},{9,13},{6,2},{2,6},{1... | collective-permute-start | bytes 884744 | tf_op jit(solution)/shard_map/ppermute | solution.py:280
  5.6 1.6 %shard_map.118.refs_1_ = bf16[144,256]{1,0:T(8,128)(2,1)} custom-call(s32[8]{0:T(128)} %lengths_ref.1, bf16[8,32,256]{2,1,0:T(8,128)(2,1)} %refs_0_.1), custom_call_target="tpu_custom_call" | custom-call | bytes 131104 | tf_op jit(solution)/shard_map/pallas_call | solution.py:23
  7.1 2.6 %collective-permute-start.3 = (bf16[144,256]{1,0:T(8,128)(2,1)}, bf16[144,256]{1,0:T(8,128)(2,1)S(1)}, u32[]{:S(2)}, u32[]{:S(2)}) collective-permute-start(bf16[144,256]{1,0:T(8,128)(2,1)} %shard_map.118.refs_1_), channel_id=1, source_target_pairs={{8,0},{12,4},{0,8},{4,12},{9,1},{13,5},{1,9},{5,13},{10,2},{14,6},... | collective-permute-start | bytes 221192 | tf_op jit(solution)/shard_map/ppermute | solution.py:188
  9.7 4.0 %collective-permute-done.3.refs_0_ = bf16[144,256]{1,0:T(8,128)(2,1)S(1)} collective-permute-done((bf16[144,256]{1,0:T(8,128)(2,1)}, bf16[144,256]{1,0:T(8,128)(2,1)S(1)}, u32[]{:S(2)}, u32[]{:S(2)}) %collective-permute-start.3) | collective-permute-done | bytes 73760 | tf_op jit(solution)/shard_map/ppermute | solution.py:188
  13.7 0.0 copy-start.6
  13.7 1.5 %collective-permute-start.4 = (bf16[144,256]{1,0:T(8,128)(2,1)S(1)}, bf16[144,256]{1,0:T(8,128)(2,1)S(1)}, u32[]{:S(2)}, u32[]{:S(2)}) collective-permute-start(bf16[144,256]{1,0:T(8,128)(2,1)S(1)} %collective-permute-done.3.refs_0_), channel_id=1, source_target_pairs={{2,0},{0,2},{3,1},{1,3},{6,4},{4,6},{7,5},{5,7},{10,8},{8,10},{11,... | collective-permute-start | bytes 221192 | tf_op jit(solution)/shard_map/ppermute | solution.py:183
  15.2 0.5 %collective-permute-start = (bf16[144,256]{1,0:T(8,128)(2,1)}, bf16[144,256]{1,0:T(8,128)(2,1)S(1)}, u32[]{:S(2)}, u32[]{:S(2)}) collective-permute-start(bf16[144,256]{1,0:T(8,128)(2,1)} %shard_map.118.refs_1_), channel_id=1, source_target_pairs={{2,0},{0,2},{3,1},{1,3},{6,4},{4,6},{7,5},{5,7},{10,8},{8,10},{11,... | collective-permute-start | bytes 221192 | tf_op jit(solution)/shard_map/ppermute | solution.py:183
  15.8 0.0 collective-permute-start.5
  15.8 2.6 %collective-permute-done.4.refs_1_ = bf16[144,256]{1,0:T(8,128)(2,1)S(1)} collective-permute-done((bf16[144,256]{1,0:T(8,128)(2,1)S(1)}, bf16[144,256]{1,0:T(8,128)(2,1)S(1)}, u32[]{:S(2)}, u32[]{:S(2)}) %collective-permute-start.4) | collective-permute-done | bytes 73760 | tf_op jit(solution)/shard_map/ppermute | solution.py:183
  18.3 0.0 copy-start.7
  18.3 0.0 collective-permute-start.6
  18.3 1.5 %collective-permute-done.refs_2_ = bf16[144,256]{1,0:T(8,128)(2,1)S(1)} collective-permute-done((bf16[144,256]{1,0:T(8,128)(2,1)}, bf16[144,256]{1,0:T(8,128)(2,1)S(1)}, u32[]{:S(2)}, u32[]{:S(2)}) %collective-permute-start) | collective-permute-done | bytes 73760 | tf_op jit(solution)/shard_map/ppermute | solution.py:183
  19.8 0.0 copy-start.4
  19.8 0.0 collective-permute-start.1
  19.8 0.0 copy-done.3
  19.8 0.7 %copy.13.refs_8_.w_task_ref = bf16[128,8]{1,0:T(8,128)(2,1)} copy(bf16[128,8]{0,1:T(8,128)(2,1)S(1)} %copy-done.3) | data formatting | bytes 4096 | tf_op args[10]
  20.5 0.0 collective-permute-done.5.refs_2_
  20.5 0.0 copy-start.8
  20.5 0.0 collective-permute-done.6.refs_3_
  20.5 0.0 copy-done.6
  20.5 0.0 copy-done.7
  20.5 0.6 %copy-done.8 = bf16[144,256]{1,0:T(8,128)(2,1)} copy-done((bf16[144,256]{1,0:T(8,128)(2,1)}, bf16[144,256]{1,0:T(8,128)(2,1)S(1)}, u32[]{:S(2)}) %copy-start.8) | copy-done | bytes 73752
  21.1 0.0 copy-start.9
  21.1 0.6 %copy-done.9 = bf16[144,256]{1,0:T(8,128)(2,1)} copy-done((bf16[144,256]{1,0:T(8,128)(2,1)}, bf16[144,256]{1,0:T(8,128)(2,1)S(1)}, u32[]{:S(2)}) %copy-start.9) | copy-done | bytes 73752
  21.8 5.2 %shard_map.122 = (bf16[64,384]{1,0:T(8,128)(2,1)}, bf16[8,64,256]{2,1,0:T(8,128)(2,1)}, bf16[8,128,64]{2,1,0:T(8,128)(2,1)}, f32[8,64,128]{2,1,0:T(8,128)}) custom-call(bf16[144,256]{1,0:T(8,128)(2,1)} %copy-done.6, bf16[144,256]{1,0:T(8,128)(2,1)} %copy-done.7, bf16[144,256]{1,0:T(8,128)(2,1)} %copy-done.8, bf16[144,256]{1,0:T(8,128)(2,1)} %copy-done.9, ...), custom_call_target="tpu_custom_call" | custom-call | flops 291504128 | bytes 919584 | tf_op jit(solution)/shard_map/pallas_call | solution.py:23
  27.0 0.0 copy-done.4
  27.0 3.3 %collective-permute-start.7 = (bf16[64,384]{1,0:T(8,128)(2,1)}, bf16[64,384]{1,0:T(8,128)(2,1)S(1)}, u32[]{:S(2)}, u32[]{:S(2)}) collective-permute-start(bf16[64,384]{1,0:T(8,128)(2,1)} %get-tuple-element.17), channel_id=1, source_target_pairs={{8,0},{12,4},{0,8},{4,12},{9,1},{13,5},{1,9},{5,13},{10,2},{14,6},... | collective-permute-start | bytes 147464 | tf_op jit(solution)/shard_map/ppermute | solution.py:188
  30.3 0.0 collective-permute-done.2.items_ref
  30.3 0.0 copy-start
  30.3 0.7 %copy-done = bf16[384,384]{1,0:T(8,128)(2,1)} copy-done((bf16[384,384]{1,0:T(8,128)(2,1)}, bf16[384,384]{1,0:T(8,128)(2,1)S(1)}, u32[]{:S(2)}) %copy-start) | copy-done | bytes 294936
  31.0 4.2 %shard_map.123 = bf16[64,384]{1,0:T(8,128)(2,1)} custom-call(bf16[384,384]{1,0:T(8,128)(2,1)} %copy-done, bf16[8,64,256]{2,1,0:T(8,128)(2,1)} %get-tuple-element.18.key_ref, bf16[8,128,64]{2,1,0:T(8,128)(2,1)} %get-tuple-element.19.pooled_ref, f32[8,64,128]{2,1,0:T(8,128)} %get-tuple-element.20.mask_ref, bf16[128,8]{1,0:T(8,128)(2,1)} %copy.13.refs_8_.w_task_ref, ...), custom_call_target="tpu_custom_call" | custom-call | flops 157286400 | bytes 952352 | tf_op jit(solution)/shard_map/pallas_call | solution.py:23
  35.2 0.0 collective-permute-start.8
  35.3 0.0 collective-permute-done.1.refs_3_
  35.3 0.0 copy-start.5
  35.3 0.6 %copy-done.5 = bf16[144,256]{1,0:T(8,128)(2,1)} copy-done((bf16[144,256]{1,0:T(8,128)(2,1)}, bf16[144,256]{1,0:T(8,128)(2,1)S(1)}, u32[]{:S(2)}) %copy-start.5) | copy-done | bytes 73752
  35.9 5.2 %shard_map.120 = (f32[8,8,384]{2,1,0:T(8,128)}, bf16[8,64,256]{2,1,0:T(8,128)(2,1)}, bf16[8,128,64]{2,1,0:T(8,128)(2,1)}, f32[8,64,128]{2,1,0:T(8,128)}) custom-call(bf16[8,32,256]{2,1,0:T(8,128)(2,1)} %refs_0_.1, bf16[144,256]{1,0:T(8,128)(2,1)} %shard_map.118.refs_1_, bf16[144,256]{1,0:T(8,128)(2,1)} %copy-done.4, bf16[144,256]{1,0:T(8,128)(2,1)} %copy-done.5, ...), custom_call_target="tpu_custom_call" | custom-call | flops 291504128 | bytes 976928 | tf_op jit(solution)/shard_map/pallas_call | solution.py:23
  41.1 4.2 %shard_map.121.refs_1_ = f32[8,8,384]{2,1,0:T(8,128)} custom-call(bf16[384,384]{1,0:T(8,128)(2,1)} %copy-done, bf16[8,64,256]{2,1,0:T(8,128)(2,1)} %get-tuple-element.14.key_ref, bf16[8,128,64]{2,1,0:T(8,128)(2,1)} %get-tuple-element.15.pooled_ref, f32[8,64,128]{2,1,0:T(8,128)} %get-tuple-element.16.mask_ref, bf16[128,8]{1,0:T(8,128)(2,1)} %copy.13.refs_8_.w_task_ref, ...), custom_call_target="tpu_custom_call" | custom-call | flops 157286400 | bytes 952352 | tf_op jit(solution)/shard_map/pallas_call | solution.py:23
  45.3 0.0 collective-permute-done.7.refs_2_
  45.3 0.0 copy-start.1
  45.3 0.0 collective-permute-done.8.refs_3_
  45.3 0.0 copy-start.2
  45.3 0.6 %copy-done.1 = bf16[64,384]{1,0:T(8,128)(2,1)} copy-done((bf16[64,384]{1,0:T(8,128)(2,1)}, bf16[64,384]{1,0:T(8,128)(2,1)S(1)}, u32[]{:S(2)}) %copy-start.1) | copy-done | bytes 49176
  45.9 0.0 copy-done.2
  46.0 1.9 %shard_map.124 = f32[8,9,8,384]{3,2,1,0:T(8,128)} custom-call(f32[8,8,384]{2,1,0:T(8,128)} %get-tuple-element.13.refs_0_, f32[8,8,384]{2,1,0:T(8,128)} %shard_map.121.refs_1_, bf16[64,384]{1,0:T(8,128)(2,1)} %copy-done.1, bf16[64,384]{1,0:T(8,128)(2,1)} %copy-done.2), custom_call_target="tpu_custom_call" | custom-call | bytes 294912 | tf_op jit(solution)/shard_map/pallas_call | solution.py:23
Async XLA Ops:
  2.5 17.3 %copy-start.3 = (bf16[128,8]{0,1:T(8,128)(2,1)S(1)}, bf16[128,8]{0,1:T(8,128)(2,1)}, u32[]{:S(2)}) copy-start(bf16[128,8]{0,1:T(8,128)(2,1)} %param.22) | copy-start | bytes 6148
  2.5 27.8 %collective-permute-start.2 = (bf16[384,384]{1,0:T(8,128)(2,1)}, bf16[384,384]{1,0:T(8,128)(2,1)S(1)}, u32[]{:S(2)}, u32[]{:S(2)}) collective-permute-start(bf16[384,384]{1,0:T(8,128)(2,1)} %shard_map.119.refs_7_), channel_id=1, source_target_pairs={{4,0},{0,4},{12,8},{8,12},{5,1},{1,5},{13,9},{9,13},{6,2},{2,6},{1... | collective-permute-start | bytes 884744 | tf_op jit(solution)/shard_map/ppermute | solution.py:280
  7.1 6.6 %collective-permute-start.3 = (bf16[144,256]{1,0:T(8,128)(2,1)}, bf16[144,256]{1,0:T(8,128)(2,1)S(1)}, u32[]{:S(2)}, u32[]{:S(2)}) collective-permute-start(bf16[144,256]{1,0:T(8,128)(2,1)} %shard_map.118.refs_1_), channel_id=1, source_target_pairs={{8,0},{12,4},{0,8},{4,12},{9,1},{13,5},{1,9},{5,13},{10,2},{14,6},... | collective-permute-start | bytes 221192 | tf_op jit(solution)/shard_map/ppermute | solution.py:188
  13.7 6.8 %copy-start.6 = (bf16[144,256]{1,0:T(8,128)(2,1)}, bf16[144,256]{1,0:T(8,128)(2,1)S(1)}, u32[]{:S(2)}) copy-start(bf16[144,256]{1,0:T(8,128)(2,1)S(1)} %collective-permute-done.3.refs_0_) | copy-start | bytes 221188
  13.7 4.6 %collective-permute-start.4 = (bf16[144,256]{1,0:T(8,128)(2,1)S(1)}, bf16[144,256]{1,0:T(8,128)(2,1)S(1)}, u32[]{:S(2)}, u32[]{:S(2)}) collective-permute-start(bf16[144,256]{1,0:T(8,128)(2,1)S(1)} %collective-permute-done.3.refs_0_), channel_id=1, source_target_pairs={{2,0},{0,2},{3,1},{1,3},{6,4},{4,6},{7,5},{5,7},{10,8},{8,10},{11,... | collective-permute-start | bytes 221192 | tf_op jit(solution)/shard_map/ppermute | solution.py:183
  15.2 4.6 %collective-permute-start = (bf16[144,256]{1,0:T(8,128)(2,1)}, bf16[144,256]{1,0:T(8,128)(2,1)S(1)}, u32[]{:S(2)}, u32[]{:S(2)}) collective-permute-start(bf16[144,256]{1,0:T(8,128)(2,1)} %shard_map.118.refs_1_), channel_id=1, source_target_pairs={{2,0},{0,2},{3,1},{1,3},{6,4},{4,6},{7,5},{5,7},{10,8},{8,10},{11,... | collective-permute-start | bytes 221192 | tf_op jit(solution)/shard_map/ppermute | solution.py:183
  15.8 4.8 %collective-permute-start.5 = (bf16[144,256]{1,0:T(8,128)(2,1)S(1)}, bf16[144,256]{1,0:T(8,128)(2,1)S(1)}, u32[]{:S(2)}, u32[]{:S(2)}) collective-permute-start(bf16[144,256]{1,0:T(8,128)(2,1)S(1)} %collective-permute-done.3.refs_0_), channel_id=1, source_target_pairs={{1,0},{0,1},{3,2},{2,3},{5,4},{4,5},{7,6},{6,7},{9,8},{8,9},{11,10... | collective-permute-start | bytes 221192 | tf_op jit(solution)/shard_map/ppermute | solution.py:183
  18.3 2.2 %copy-start.7 = (bf16[144,256]{1,0:T(8,128)(2,1)}, bf16[144,256]{1,0:T(8,128)(2,1)S(1)}, u32[]{:S(2)}) copy-start(bf16[144,256]{1,0:T(8,128)(2,1)S(1)} %collective-permute-done.4.refs_1_) | copy-start | bytes 221188
  18.3 2.2 %collective-permute-start.6 = (bf16[144,256]{1,0:T(8,128)(2,1)S(1)}, bf16[144,256]{1,0:T(8,128)(2,1)S(1)}, u32[]{:S(2)}, u32[]{:S(2)}) collective-permute-start(bf16[144,256]{1,0:T(8,128)(2,1)S(1)} %collective-permute-done.4.refs_1_), channel_id=1, source_target_pairs={{1,0},{0,1},{3,2},{2,3},{5,4},{4,5},{7,6},{6,7},{9,8},{8,9},{11,10... | collective-permute-start | bytes 221192 | tf_op jit(solution)/shard_map/ppermute | solution.py:183
  19.8 7.2 %copy-start.4 = (bf16[144,256]{1,0:T(8,128)(2,1)}, bf16[144,256]{1,0:T(8,128)(2,1)S(1)}, u32[]{:S(2)}) copy-start(bf16[144,256]{1,0:T(8,128)(2,1)S(1)} %collective-permute-done.refs_2_) | copy-start | bytes 221188
  19.8 15.5 %collective-permute-start.1 = (bf16[144,256]{1,0:T(8,128)(2,1)S(1)}, bf16[144,256]{1,0:T(8,128)(2,1)S(1)}, u32[]{:S(2)}, u32[]{:S(2)}) collective-permute-start(bf16[144,256]{1,0:T(8,128)(2,1)S(1)} %collective-permute-done.refs_2_), channel_id=1, source_target_pairs={{1,0},{0,1},{3,2},{2,3},{5,4},{4,5},{7,6},{6,7},{9,8},{8,9},{11,10... | collective-permute-start | bytes 221192 | tf_op jit(solution)/shard_map/ppermute | solution.py:183
  20.5 0.6 %copy-start.8 = (bf16[144,256]{1,0:T(8,128)(2,1)}, bf16[144,256]{1,0:T(8,128)(2,1)S(1)}, u32[]{:S(2)}) copy-start(bf16[144,256]{1,0:T(8,128)(2,1)S(1)} %collective-permute-done.5.refs_2_) | copy-start | bytes 221188
  21.1 0.6 %copy-start.9 = (bf16[144,256]{1,0:T(8,128)(2,1)}, bf16[144,256]{1,0:T(8,128)(2,1)S(1)}, u32[]{:S(2)}) copy-start(bf16[144,256]{1,0:T(8,128)(2,1)S(1)} %collective-permute-done.6.refs_3_) | copy-start | bytes 221188
  27.0 18.3 %collective-permute-start.7 = (bf16[64,384]{1,0:T(8,128)(2,1)}, bf16[64,384]{1,0:T(8,128)(2,1)S(1)}, u32[]{:S(2)}, u32[]{:S(2)}) collective-permute-start(bf16[64,384]{1,0:T(8,128)(2,1)} %get-tuple-element.17), channel_id=1, source_target_pairs={{8,0},{12,4},{0,8},{4,12},{9,1},{13,5},{1,9},{5,13},{10,2},{14,6},... | collective-permute-start | bytes 147464 | tf_op jit(solution)/shard_map/ppermute | solution.py:188
  30.3 0.7 %copy-start = (bf16[384,384]{1,0:T(8,128)(2,1)}, bf16[384,384]{1,0:T(8,128)(2,1)S(1)}, u32[]{:S(2)}) copy-start(bf16[384,384]{1,0:T(8,128)(2,1)S(1)} %collective-permute-done.2.items_ref) | copy-start | bytes 884740
  35.2 10.1 %collective-permute-start.8 = (bf16[64,384]{1,0:T(8,128)(2,1)}, bf16[64,384]{1,0:T(8,128)(2,1)S(1)}, u32[]{:S(2)}, u32[]{:S(2)}) collective-permute-start(bf16[64,384]{1,0:T(8,128)(2,1)} %shard_map.123), channel_id=1, source_target_pairs={{8,0},{12,4},{0,8},{4,12},{9,1},{13,5},{1,9},{5,13},{10,2},{14,6},... | collective-permute-start | bytes 147464 | tf_op jit(solution)/shard_map/ppermute | solution.py:188
  35.3 0.6 %copy-start.5 = (bf16[144,256]{1,0:T(8,128)(2,1)}, bf16[144,256]{1,0:T(8,128)(2,1)S(1)}, u32[]{:S(2)}) copy-start(bf16[144,256]{1,0:T(8,128)(2,1)S(1)} %collective-permute-done.1.refs_3_) | copy-start | bytes 221188
  45.3 0.6 %copy-start.1 = (bf16[64,384]{1,0:T(8,128)(2,1)}, bf16[64,384]{1,0:T(8,128)(2,1)S(1)}, u32[]{:S(2)}) copy-start(bf16[64,384]{1,0:T(8,128)(2,1)S(1)} %collective-permute-done.7.refs_2_) | copy-start | bytes 147460
  45.3 0.6 %copy-start.2 = (bf16[64,384]{1,0:T(8,128)(2,1)}, bf16[64,384]{1,0:T(8,128)(2,1)S(1)}, u32[]{:S(2)}) copy-start(bf16[64,384]{1,0:T(8,128)(2,1)S(1)} %collective-permute-done.8.refs_3_) | copy-start | bytes 147460

commit v2 on v1

--- a/solution.py
+++ b/solution.py
@@ -18,8 +18,13 @@
 ANY = pl.BlockSpec(memory_space=pl.ANY)
 
 
+def near(array):
+    return pltpu.with_memory_space_constraint(array, pltpu.VMEM)
+
+
 def call(kernel, out_shape, in_specs, out_specs, args, flops, scratch=()):
     moved = sum(math.prod(a.shape) * a.dtype.itemsize for a in args)
+    args = [near(a) if spec is VMEM else a for a, spec in zip(args, in_specs)]
     return pl.pallas_call(
         kernel,
         out_shape=out_shape,
@@ -53,42 +58,42 @@
     out_ref[width:, :] = terms.T.astype(BF16)
 
 
-def keys_values(pieces, w_key_ref, w_value_ref, w_pooled_ref, key_ref, pooled_ref, mask_ref, turn):
-    users, count, width = key_ref.shape
+def keys_values(pieces, turn, w_key_ref, w_value_ref, w_pooled_ref, key_ref, pooled_ref, mask_ref, history_ref):
+    pairs, _, both = pooled_ref.shape
+    full = both // 2
+    users = 2 * pairs
     share = users // len(pieces)
-    w_pooled = w_pooled_ref[...].astype(F32).T.astype(BF16)
     for s, parts in enumerate(pieces):
-        tokens = count // len(parts)
-        lengths = turn[s]
+        tokens = full // len(parts)
         for r, (rows, first) in enumerate(parts):
-            keys = jnp.dot(rows, w_key_ref[...], preferred_element_type=F32).astype(BF16)
-            values = jnp.dot(rows, w_value_ref[...], preferred_element_type=F32).astype(BF16)
-            place = slice(r * tokens, (r + 1) * tokens)
-            at = lax.broadcasted_iota(jnp.int32, (tokens, 128), 0) + first
-            at = at.astype(F32)
+            at = (lax.broadcasted_iota(jnp.int32, (tokens, 128), 0) + first).astype(F32)
             for u in range(share):
-                user = s * share + u
-                key_ref[user, place, :] = keys[u * tokens : (u + 1) * tokens]
-                pooled = lax.dot_general(
-                    w_pooled,
-                    values[u * tokens : (u + 1) * tokens],
-                    (((1,), (1,)), ((), ())),
-                    preferred_element_type=F32,
-                )
-                pooled_ref[user, :, place] = pooled.astype(BF16)
-                mask_ref[user, place, :] = jnp.where(at < lengths[u : u + 1, :128], 0.0, -jnp.inf)
-
-
-def score(items_ref, key_ref, pooled_ref, mask_ref, w_task_ref, bias_task_ref, out_ref, shares):
-    users, _, width = key_ref.shape
-    tasks = w_task_ref.shape[1]
-    hid = w_task_ref.shape[0]
-    share = users // shares
+                start = (s * share + u) * full + r * tokens
+                place = slice(start, start + tokens)
+                history_ref[place, :] = rows[u * tokens : (u + 1) * tokens]
+                mask_ref[place, :] = jnp.where(at < turn[s][u : u + 1, :128], 0.0, -jnp.inf)
+    key_ref[...] = jnp.dot(history_ref[...], w_key_ref[...], preferred_element_type=F32).astype(BF16)
+    values = jnp.dot(history_ref[...], w_value_ref[...], preferred_element_type=F32).astype(BF16)
+    pooled = jnp.dot(values, w_pooled_ref[...], preferred_element_type=F32)
+    hid = pooled.shape[1]
+    lane = lax.broadcasted_iota(jnp.int32, (hid, both), 1)
+    for pair in range(pairs):
+        flat = pooled[pair * both : (pair + 1) * both].T
+        pooled_ref[pair, :hid, :] = jnp.where(lane < full, flat, 0.0).astype(BF16)
+        pooled_ref[pair, hid:, :] = jnp.where(lane < full, 0.0, flat).astype(BF16)
+
+
+def score(items_ref, state, w_task_ref, bias_task_ref, out_ref, scratch, shares):
+    key_ref, pooled_ref, mask_ref = state
+    scores_ref, weights_ref, hidden_ref = scratch
+    width = key_ref.shape[1]
+    tasks, hid = w_task_ref.shape
+    pairs, _, both = pooled_ref.shape
+    full = both // 2
+    share = pairs // shares
+    columns = items_ref.shape[1]
     factor = math.log2(math.e) / math.sqrt(width)
-    queries = items_ref[:width, :]
-    terms = items_ref[width:, :].astype(F32)
-    columns = terms.shape[1]
-    w_task = w_task_ref[...].astype(F32).T
+    w_task = w_task_ref[...].astype(F32)
     blank = jnp.zeros_like(w_task)
     heads = jnp.concatenate(
         [jnp.concatenate([w_task, blank], 1), jnp.concatenate([blank, w_task], 1)], 0
@@ -98,27 +103,32 @@
     for task in range(tasks):
         bias = jnp.where(row % tasks == task, bias_task_ref[task], bias)
 
-    def hidden(user):
-        scores = jnp.dot(key_ref[user], queries, preferred_element_type=F32)
-        mask = mask_ref[user]
-        scores = scores + jnp.concatenate([mask] * (columns // 128), 1)
-        maximum = jnp.max(scores, axis=0, keepdims=True)
-        expo = jnp.exp2((scores - maximum) * factor)
-        weights = (expo * (1.0 / jnp.sum(expo, axis=0, keepdims=True))).astype(BF16)
-        total = jnp.dot(pooled_ref[user], weights, preferred_element_type=F32) + terms
-        return jnp.maximum(total, 0.0).astype(BF16)
-
-    for s in range(shares):
-        first = lax.rem(lax.axis_index("sub") + s, shares) * share
-        for u in range(0, share, 2):
-            both = jnp.concatenate([hidden(s * share + u), hidden(s * share + u + 1)], 0)
-            logits = jnp.dot(heads, both, preferred_element_type=F32) + bias
-            if len(out_ref.shape) == 3:
-                out_ref[first + u] = logits[:tasks]
-                out_ref[first + u + 1] = logits[tasks:]
-            else:
-                place = pl.multiple_of((first + u) * tasks, 2 * tasks)
-                out_ref[pl.ds(place, 2 * tasks), :] = logits.astype(out_ref.dtype)
+    scores_ref[...] = jnp.dot(key_ref[...], items_ref[:width, :], preferred_element_type=F32)
+    for user in range(2 * pairs):
+        rows = slice(user * full, (user + 1) * full)
+        for column in range(0, columns, 128):
+            lanes = slice(column, column + 128)
+            scores = scores_ref[rows, lanes] + mask_ref[rows, :]
+            maximum = jnp.max(scores, axis=0, keepdims=True)
+            expo = jnp.exp2((scores - maximum) * factor)
+            weights = expo * (1.0 / jnp.sum(expo, axis=0, keepdims=True))
+            weights_ref[rows, lanes] = weights.astype(BF16)
+    for pair in range(pairs):
+        rows = slice(pair * both, (pair + 1) * both)
+        total = jnp.dot(pooled_ref[pair], weights_ref[rows, :], preferred_element_type=F32)
+        for user in range(2):
+            part = slice(user * hid, (user + 1) * hid)
+            hidden = total[part] + items_ref[width:, :].astype(F32)
+            hidden_ref[pair, part, :] = jnp.maximum(hidden, 0.0).astype(BF16)
+    for pair in range(pairs):
+        logits = jnp.dot(heads, hidden_ref[pair], preferred_element_type=F32) + bias
+        first = lax.rem(lax.axis_index("sub") + pair // share, shares) * share + pair % share
+        if len(out_ref.shape) == 3:
+            out_ref[2 * first] = logits[:tasks]
+            out_ref[2 * first + 1] = logits[tasks:]
+        else:
+            place = pl.multiple_of(2 * first * tasks, 2 * tasks)
+            out_ref[pl.ds(place, 2 * tasks), :] = logits.astype(out_ref.dtype)
 
 
 def first_kernel(own, shares, parts, *refs):
@@ -129,10 +139,11 @@
     sent, refs = list(refs[:count]), refs[count:]
     piece_refs = [None if local else sent.pop(0) for local in given]
     w_key_ref, w_value_ref, w_pooled_ref, items_ref, w_task_ref, bias_task_ref = refs[:6]
-    out_ref, key_ref, pooled_ref, mask_ref = refs[6:]
+    out_ref, key_ref, pooled_ref, mask_ref, rows_ref, *scratch = refs[6:]
     me, side = lax.axis_index("users"), lax.axis_index("sub")
     pieces, turn = [], []
     rows = piece_refs[0].shape[0] - LENGTH_ROWS
+    tokens = pooled_ref.shape[2] // 2 // parts
     for s in range(shares):
         entries = []
         for r in range(parts):
@@ -143,16 +154,17 @@
                 content = chosen.reshape(rows, history_ref.shape[2])
             else:
                 content = ref[:rows, :]
-            tokens = key_ref.shape[1] // parts
             entries.append((content, lax.rem(me + r, parts) * tokens))
         pieces.append(entries)
         turn.append(piece_refs[s * parts + parts - 1][rows:, :].astype(F32))
-    keys_values(pieces, w_key_ref, w_value_ref, w_pooled_ref, key_ref, pooled_ref, mask_ref, turn)
-    score(items_ref, key_ref, pooled_ref, mask_ref, w_task_ref, bias_task_ref, out_ref, shares)
-
-
-def next_kernel(shares, items_ref, key_ref, pooled_ref, mask_ref, w_task_ref, bias_task_ref, out_ref):
-    score(items_ref, key_ref, pooled_ref, mask_ref, w_task_ref, bias_task_ref, out_ref, shares)
+    state = (key_ref, pooled_ref, mask_ref)
+    keys_values(pieces, turn, w_key_ref, w_value_ref, w_pooled_ref, *state, rows_ref)
+    score(items_ref, state, w_task_ref, bias_task_ref, out_ref, scratch, shares)
+
+
+def next_kernel(shares, items_ref, key_ref, pooled_ref, mask_ref, w_task_ref, bias_task_ref, out_ref, *scratch):
+    state = (key_ref, pooled_ref, mask_ref)
+    score(items_ref, state, w_task_ref, bias_task_ref, out_ref, scratch, shares)
 
 
 def place_kernel(count, *refs):
@@ -219,7 +231,7 @@
 
     piece = call(
         pack_kernel,
-        jax.ShapeDtypeStruct((users // shares * tokens + LENGTH_ROWS, width), BF16),
+        pltpu.VMEM((users // shares * tokens + LENGTH_ROWS, width), BF16),
         [SMEM, VMEM],
         VMEM,
         (lengths, history),
@@ -227,7 +239,7 @@
     )
     mine = call(
         project_kernel,
-        jax.ShapeDtypeStruct((width + hid, items), BF16),
+        pltpu.VMEM((width + hid, items), BF16),
         [VMEM] * 5,
         VMEM,
         (item_rows, w_query, w_item, w_joint, bias_hidden[None]),
@@ -235,12 +247,17 @@
     )
     flops = 2 * users * items * (full * (width + hid) + hid * tasks)
     state = (
-        jax.ShapeDtypeStruct((users, full, width), BF16),
-        jax.ShapeDtypeStruct((users, hid, full), BF16),
-        jax.ShapeDtypeStruct((users, full, 128), F32),
-    )
-    kept = jax.ShapeDtypeStruct((users, tasks, items), F32)
-    sent = jax.ShapeDtypeStruct((users * tasks, items), BF16)
+        pltpu.VMEM((users * full, width), BF16),
+        pltpu.VMEM((users // 2, 2 * hid, 2 * full), BF16),
+        pltpu.VMEM((users * full, 128), F32),
+    )
+    kept = pltpu.VMEM((users, tasks, items), F32)
+    sent = pltpu.VMEM((users * tasks, items), BF16)
+    scratch = (
+        pltpu.VMEM((users * full, items), F32),
+        pltpu.VMEM((users * full, items), BF16),
+        pltpu.VMEM((users // 2, 2 * hid, items), BF16),
+    )
 
     def start(table, block, out, own):
         flat = [entry for row in table for entry in row if entry is not None]
@@ -250,8 +267,9 @@
             (out, *state),
             [VMEM] * (len(head) + len(flat) + 5) + [SMEM],
             [VMEM] * 4,
-            (*head, *flat, w_key, w_value, w_pooled, block, w_task, bias_task),
+            (*head, *flat, w_key, w_value, w_pooled, block, w_task.T, bias_task),
             flops + 4 * users * full * width * width,
+            (pltpu.VMEM((users * full, width), BF16), *scratch),
         )
         return result[0], result[1:]
 
@@ -261,8 +279,9 @@
             out,
             [VMEM] * 5 + [SMEM],
             VMEM,
-            (block, *held, w_task, bias_task),
+            (block, *held, w_task.T, bias_task),
             flops,
+            scratch,
         )
 
     if count % 2 or count > WIN:
@@ -281,8 +300,8 @@
     at_home, held = start(own, mine, kept, True)
     away = []
     for ahead, entry in enumerate(far, 1):
-        near, guests = start(spread(entry, shares, parts), mine, sent, False)
-        back = [from_pair(near, -ahead)]
+        result, guests = start(spread(entry, shares, parts), mine, sent, False)
+        back = [from_pair(result, -ahead)]
         back.append(from_pair(go_on(guests, other, sent), -ahead))
         away.append(back)
     beside = go_on(held, other, kept)

time: 48.3 us -> 35.6 us (0.74)
  Pallas kernels: 24.9 us -> 8.72 us
  waiting for transfers between devices: 8.05 us -> 10.8 us
  local copies, waits for them, and re-layouts: 3.89 us -> 4.41 us
    pallas_call x7, Pallas kernels: 24.9 us -> 8.72 us  [call(): pl.pallas_call(kernel, out_shape=out_shape, in_specs=in_specs, out_specs=...]
    ppermute x3, waiting for transfers between devices: 4.02 us -> 6.94 us  [from_pair(): lax.ppermute(block, 'blk', [((i + 2 * distance) % count, i) for i in rang...]
    unnamed x21 -> x20, local copies, waits for them, and re-layouts: 3.89 us -> 4.41 us
  transfers between devices with their start and end apart: 9 -> 9, of which waited for: 3 -> 4; matrix products, arithmetic and copies ran while one was open for 1% -> 0% of each run, Pallas kernels for 43% -> 20%
where the time goes in v2:
time: 35.6 us; the launch traced here: 35.3 us
  starting transfers between devices  11.3 us (32%)
  waiting for transfers between devices  10.8 us (30%)
  Pallas kernels  8.72 us (24%)
  local copies, waits for them, and re-layouts  4.41 us (12%)
    pallas_call x7, Pallas kernels, call(): pl.pallas_call(kernel, out_shape=out_shape, in_specs=in_specs, out_specs=...  8.72 us
    ppermute x3, waiting for transfers between devices, from_pair(): lax.ppermute(block, 'blk', [((i + 2 * distance) % count, i) for i in rang...  6.94 us
    ppermute x3, starting transfers between devices, from_pair(): lax.ppermute(block, 'blk', [((i + 2 * distance) % count, i) for i in rang...  6.13 us
    unnamed x20, local copies, waits for them, and re-layouts  4.41 us
    ppermute x5, waiting for transfers between devices, shift(): lax.ppermute(block, axis, [((i + distance) % count, i) for i in range(cou...  3.81 us
    ppermute x1, starting transfers between devices, shards(): other = lax.ppermute(mine, 'blk', [(i ^ 1, i) for i in range(count)])  3.12 us
    ppermute x5, starting transfers between devices, shift(): lax.ppermute(block, axis, [((i + distance) % count, i) for i in range(cou...  2.03 us
  transfers between devices with their start and end apart: 9, of which 4 were waited for; matrix products, arithmetic and copies ran while one was open for 0% of the time, Pallas kernels for 20%

profile of v2, /device:TPU:0, one launch (start us, length us, event | category | flops | bytes accessed | tf_op | source)
XLA Modules:
  0.0 35.3 jit_solution(10069306935151820416)
XLA Ops:
  0.0 0.0 copy-start.6
  0.0 0.7 %copy-done.6 = f32[128]{0:T(128)S(1)} copy-done((f32[128]{0:T(128)S(1)}, f32[128]{0:T(128)}, u32[]{:S(2)}) %copy-start.6) | copy-done | bytes 536
  0.7 0.0 copy-start
  0.7 1.0 %copy-done = bf16[384,512]{1,0:T(8,128)(2,1)S(1)} copy-done((bf16[384,512]{1,0:T(8,128)(2,1)S(1)}, bf16[384,512]{1,0:T(8,128)(2,1)}, u32[]{:S(2)}) %copy-start) | copy-done | bytes 393240
  1.7 0.0 copy-start.1
  1.7 0.9 %copy-done.1 = bf16[512,256]{1,0:T(8,128)(2,1)S(1)} copy-done((bf16[512,256]{1,0:T(8,128)(2,1)S(1)}, bf16[512,256]{1,0:T(8,128)(2,1)}, u32[]{:S(2)}) %copy-start.1) | copy-done | bytes 262168
  2.6 0.0 copy-start.2
  2.6 0.9 %copy-done.2 = bf16[512,256]{1,0:T(8,128)(2,1)S(1)} copy-done((bf16[512,256]{1,0:T(8,128)(2,1)S(1)}, bf16[512,256]{1,0:T(8,128)(2,1)}, u32[]{:S(2)}) %copy-start.2) | copy-done | bytes 262168
  3.6 0.0 copy-start.4
  3.6 0.8 %copy-done.4 = bf16[256,128]{1,0:T(8,128)(2,1)S(1)} copy-done((bf16[256,128]{1,0:T(8,128)(2,1)S(1)}, bf16[256,128]{1,0:T(8,128)(2,1)}, u32[]{:S(2)}) %copy-start.4) | copy-done | bytes 65560
  4.4 0.0 copy-start.3
  4.4 0.0 copy-start.8
  4.4 0.6 %shard_map.119.refs_7_ = bf16[384,384]{1,0:T(8,128)(2,1)S(1)} custom-call(bf16[384,512]{1,0:T(8,128)(2,1)S(1)} %copy-done, bf16[512,256]{1,0:T(8,128)(2,1)S(1)} %copy-done.1, bf16[512,256]{1,0:T(8,128)(2,1)S(1)} %copy-done.2, bf16[256,128]{1,0:T(8,128)(2,1)S(1)} %copy-done.4, f32[1,128]{1,0:T(1,128)S(1)} %bitcast.6), custom_call_target="tpu_custom_call" | custom-call | flops 201326592 | bytes 983552 | tf_op jit(solution)/shard_map/pallas_call | solution.py:28
  5.0 0.0 copy-start.5
  5.0 0.0 copy-start.7
  5.0 0.0 copy-start.9
  5.1 3.1 %collective-permute-start.2 = (bf16[384,384]{1,0:T(8,128)(2,1)S(1)}, bf16[384,384]{1,0:T(8,128)(2,1)S(1)}, u32[]{:S(2)}, u32[]{:S(2)}) collective-permute-start(bf16[384,384]{1,0:T(8,128)(2,1)S(1)} %shard_map.119.refs_7_), channel_id=1, source_target_pairs={{4,0},{0,4},{12,8},{8,12},{5,1},{1,5},{13,9},{9,13},{6,2},{2,6},{1... | collective-permute-start | bytes 884744 | tf_op jit(solution)/shard_map/ppermute | solution.py:299
  8.2 0.0 copy-done.3
  8.2 0.7 %shard_map.118.refs_1_ = bf16[144,256]{1,0:T(8,128)(2,1)S(1)} custom-call(s32[8]{0:T(128)} %lengths_ref.1, bf16[8,32,256]{2,1,0:T(8,128)(2,1)S(1)} %copy-done.3), custom_call_target="tpu_custom_call" | custom-call | bytes 131104 | tf_op jit(solution)/shard_map/pallas_call | solution.py:28
  8.9 2.7 %collective-permute-start.3 = (bf16[144,256]{1,0:T(8,128)(2,1)S(1)}, bf16[144,256]{1,0:T(8,128)(2,1)S(1)}, u32[]{:S(2)}, u32[]{:S(2)}) collective-permute-start(bf16[144,256]{1,0:T(8,128)(2,1)S(1)} %shard_map.118.refs_1_), channel_id=1, source_target_pairs={{8,0},{12,4},{0,8},{4,12},{9,1},{13,5},{1,9},{5,13},{10,2},{14,6},... | collective-permute-start | bytes 221192 | tf_op jit(solution)/shard_map/ppermute | solution.py:200
  11.5 4.5 %collective-permute-done.3.refs_0_ = bf16[144,256]{1,0:T(8,128)(2,1)S(1)} collective-permute-done((bf16[144,256]{1,0:T(8,128)(2,1)S(1)}, bf16[144,256]{1,0:T(8,128)(2,1)S(1)}, u32[]{:S(2)}, u32[]{:S(2)}) %collective-permute-start.3) | collective-permute-done | bytes 73760 | tf_op jit(solution)/shard_map/ppermute | solution.py:200
  16.0 1.5 %collective-permute-start.4 = (bf16[144,256]{1,0:T(8,128)(2,1)S(1)}, bf16[144,256]{1,0:T(8,128)(2,1)S(1)}, u32[]{:S(2)}, u32[]{:S(2)}) collective-permute-start(bf16[144,256]{1,0:T(8,128)(2,1)S(1)} %collective-permute-done.3.refs_0_), channel_id=1, source_target_pairs={{2,0},{0,2},{3,1},{1,3},{6,4},{4,6},{7,5},{5,7},{10,8},{8,10},{11,... | collective-permute-start | bytes 221192 | tf_op jit(solution)/shard_map/ppermute | solution.py:195
  17.5 0.5 %collective-permute-start = (bf16[144,256]{1,0:T(8,128)(2,1)S(1)}, bf16[144,256]{1,0:T(8,128)(2,1)S(1)}, u32[]{:S(2)}, u32[]{:S(2)}) collective-permute-start(bf16[144,256]{1,0:T(8,128)(2,1)S(1)} %shard_map.118.refs_1_), channel_id=1, source_target_pairs={{2,0},{0,2},{3,1},{1,3},{6,4},{4,6},{7,5},{5,7},{10,8},{8,10},{11,... | collective-permute-start | bytes 221192 | tf_op jit(solution)/shard_map/ppermute | solution.py:195
  18.0 0.0 collective-permute-start.5
  18.0 2.3 %collective-permute-done.4.refs_1_ = bf16[144,256]{1,0:T(8,128)(2,1)S(1)} collective-permute-done((bf16[144,256]{1,0:T(8,128)(2,1)S(1)}, bf16[144,256]{1,0:T(8,128)(2,1)S(1)}, u32[]{:S(2)}, u32[]{:S(2)}) %collective-permute-start.4) | collective-permute-done | bytes 73760 | tf_op jit(solution)/shard_map/ppermute | solution.py:195
  20.4 0.0 collective-permute-start.6
  20.4 1.5 %collective-permute-done.refs_2_ = bf16[144,256]{1,0:T(8,128)(2,1)S(1)} collective-permute-done((bf16[144,256]{1,0:T(8,128)(2,1)S(1)}, bf16[144,256]{1,0:T(8,128)(2,1)S(1)}, u32[]{:S(2)}, u32[]{:S(2)}) %collective-permute-start) | collective-permute-done | bytes 73760 | tf_op jit(solution)/shard_map/ppermute | solution.py:195
  21.9 0.0 collective-permute-start.1
  21.9 0.0 collective-permute-done.5.refs_2_
  21.9 0.0 collective-permute-done.6.refs_3_
  21.9 0.0 copy-done.8
  21.9 0.0 copy-done.5
  21.9 0.0 copy-done.7
  21.9 0.0 copy-done.9
  21.9 1.7 %shard_map.122 = (bf16[64,384]{1,0:T(8,128)(2,1)S(1)}, bf16[512,256]{1,0:T(8,128)(2,1)S(1)}, bf16[4,256,128]{2,1,0:T(8,128)(2,1)S(1)}, f32[512,128]{1,0:T(8,128)S(1)}) custom-call(bf16[144,256]{1,0:T(8,128)(2,1)S(1)} %collective-permute-done.3.refs_0_, bf16[144,256]{1,0:T(8,128)(2,1)S(1)} %collective-permute-done.4.refs_1_, ...), custom_call_target="tpu_custom_call" | custom-call | flops 291504128 | bytes 919584 | tf_op jit(solution)/shard_map/pallas_call | solution.py:28
  23.6 3.4 %collective-permute-start.7 = (bf16[64,384]{1,0:T(8,128)(2,1)S(1)}, bf16[64,384]{1,0:T(8,128)(2,1)S(1)}, u32[]{:S(2)}, u32[]{:S(2)}) collective-permute-start(bf16[64,384]{1,0:T(8,128)(2,1)S(1)} %get-tuple-element.17), channel_id=1, source_target_pairs={{8,0},{12,4},{0,8},{4,12},{9,1},{13,5},{1,9},{5,13},{10,2},{14,6},... | collective-permute-start | bytes 147464 | tf_op jit(solution)/shard_map/ppermute | solution.py:200
  27.0 0.0 collective-permute-done.2.items_ref
  27.0 1.5 %shard_map.123 = bf16[64,384]{1,0:T(8,128)(2,1)S(1)} custom-call(bf16[384,384]{1,0:T(8,128)(2,1)S(1)} %collective-permute-done.2.items_ref, bf16[512,256]{1,0:T(8,128)(2,1)S(1)} %get-tuple-element.18.key_ref, bf16[4,256,128]{2,1,0:T(8,128)(2,1)S(1)} %get-tuple-element.19.pooled_ref, f32[512,128]{1,0:T(8,128)S(1)} %get-tuple-element.20.mask_ref, ...), custom_call_target="tpu_custom_call" | custom-call | flops 157286400 | bytes 1083424 | tf_op jit(solution)/shard_map/pallas_call | solution.py:28
  28.5 0.1 collective-permute-start.8
  28.6 0.0 collective-permute-done.1.refs_3_
  28.6 1.7 %shard_map.120 = (f32[8,8,384]{2,1,0:T(8,128)S(1)}, bf16[512,256]{1,0:T(8,128)(2,1)S(1)}, bf16[4,256,128]{2,1,0:T(8,128)(2,1)S(1)}, f32[512,128]{1,0:T(8,128)S(1)}) custom-call(bf16[8,32,256]{2,1,0:T(8,128)(2,1)S(1)} %copy-done.3, bf16[144,256]{1,0:T(8,128)(2,1)S(1)} %shard_map.118.refs_1_, bf16[144,256]{1,0:T(8,128)(2,1)S(1)} %collective-permute-done.refs_2_, ...), custom_call_target="tpu_custom_call" | custom-call | flops 291504128 | bytes 976928 | tf_op jit(solution)/shard_map/pallas_call | solution.py:28
  30.3 1.5 %shard_map.121.refs_1_ = f32[8,8,384]{2,1,0:T(8,128)S(1)} custom-call(bf16[384,384]{1,0:T(8,128)(2,1)S(1)} %collective-permute-done.2.items_ref, bf16[512,256]{1,0:T(8,128)(2,1)S(1)} %get-tuple-element.14.key_ref, bf16[4,256,128]{2,1,0:T(8,128)(2,1)S(1)} %get-tuple-element.15.pooled_ref, f32[512,128]{1,0:T(8,128)S(1)} %get-tuple-element.16.mask_ref, ...), custom_call_target="tpu_custom_call" | custom-call | flops 157286400 | bytes 1083424 | tf_op jit(solution)/shard_map/pallas_call | solution.py:28
  31.8 0.0 collective-permute-done.7.refs_2_
  31.8 2.4 %collective-permute-done.8.refs_3_ = bf16[64,384]{1,0:T(8,128)(2,1)S(1)} collective-permute-done((bf16[64,384]{1,0:T(8,128)(2,1)S(1)}, bf16[64,384]{1,0:T(8,128)(2,1)S(1)}, u32[]{:S(2)}, u32[]{:S(2)}) %collective-permute-start.8) | collective-permute-done | bytes 49184 | tf_op jit(solution)/shard_map/ppermute | solution.py:200
  34.3 1.0 %shard_map.124 = f32[8,9,8,384]{3,2,1,0:T(8,128)} custom-call(f32[8,8,384]{2,1,0:T(8,128)S(1)} %get-tuple-element.13.refs_0_, f32[8,8,384]{2,1,0:T(8,128)S(1)} %shard_map.121.refs_1_, bf16[64,384]{1,0:T(8,128)(2,1)S(1)} %collective-permute-done.7.refs_2_, bf16[64,384]{1,0:T(8,128)(2,1)S(1)} %collective-permute-done.8.refs_3_), custom_call_target="tpu_custom_call" | custom-call | bytes 294912 | tf_op jit(solution)/shard_map/pallas_call | solution.py:28
Async XLA Ops:
  0.0 0.7 %copy-start.6 = (f32[128]{0:T(128)S(1)}, f32[128]{0:T(128)}, u32[]{:S(2)}) copy-start(f32[128]{0:T(128)} %param.21) | copy-start | bytes 1540
  0.7 1.0 %copy-start = (bf16[384,512]{1,0:T(8,128)(2,1)S(1)}, bf16[384,512]{1,0:T(8,128)(2,1)}, u32[]{:S(2)}) copy-start(bf16[384,512]{1,0:T(8,128)(2,1)} %items_ref.1) | copy-start | bytes 1179652
  1.7 0.9 %copy-start.1 = (bf16[512,256]{1,0:T(8,128)(2,1)S(1)}, bf16[512,256]{1,0:T(8,128)(2,1)}, u32[]{:S(2)}) copy-start(bf16[512,256]{1,0:T(8,128)(2,1)} %w_query_ref.1) | copy-start | bytes 786436
  2.6 0.9 %copy-start.2 = (bf16[512,256]{1,0:T(8,128)(2,1)S(1)}, bf16[512,256]{1,0:T(8,128)(2,1)}, u32[]{:S(2)}) copy-start(bf16[512,256]{1,0:T(8,128)(2,1)} %w_item_ref.1) | copy-start | bytes 786436
  3.6 0.8 %copy-start.4 = (bf16[256,128]{1,0:T(8,128)(2,1)S(1)}, bf16[256,128]{1,0:T(8,128)(2,1)}, u32[]{:S(2)}) copy-start(bf16[256,128]{1,0:T(8,128)(2,1)} %w_joint_ref.1) | copy-start | bytes 196612
  4.4 3.8 %copy-start.3 = (bf16[8,32,256]{2,1,0:T(8,128)(2,1)S(1)}, bf16[8,32,256]{2,1,0:T(8,128)(2,1)}, u32[]{:S(2)}) copy-start(bf16[8,32,256]{2,1,0:T(8,128)(2,1)} %refs_0_.1) | copy-start | bytes 393220
  4.4 17.5 %copy-start.8 = (bf16[256,256]{1,0:T(8,128)(2,1)S(1)}, bf16[256,256]{1,0:T(8,128)(2,1)}, u32[]{:S(2)}) copy-start(bf16[256,256]{1,0:T(8,128)(2,1)} %refs_5_.3) | copy-start | bytes 393220
  5.0 16.9 %copy-start.5 = (bf16[128,8]{0,1:T(8,128)(2,1)S(1)}, bf16[128,8]{0,1:T(8,128)(2,1)}, u32[]{:S(2)}) copy-start(bf16[128,8]{0,1:T(8,128)(2,1)} %param.22) | copy-start | bytes 6148
  5.0 16.9 %copy-start.7 = (bf16[256,256]{1,0:T(8,128)(2,1)S(1)}, bf16[256,256]{1,0:T(8,128)(2,1)}, u32[]{:S(2)}) copy-start(bf16[256,256]{1,0:T(8,128)(2,1)} %refs_4_.3) | copy-start | bytes 393220
  5.0 16.9 %copy-start.9 = (bf16[256,128]{1,0:T(8,128)(2,1)S(1)}, bf16[256,128]{1,0:T(8,128)(2,1)}, u32[]{:S(2)}) copy-start(bf16[256,128]{1,0:T(8,128)(2,1)} %refs_6_.3) | copy-start | bytes 196612
  5.1 22.0 %collective-permute-start.2 = (bf16[384,384]{1,0:T(8,128)(2,1)S(1)}, bf16[384,384]{1,0:T(8,128)(2,1)S(1)}, u32[]{:S(2)}, u32[]{:S(2)}) collective-permute-start(bf16[384,384]{1,0:T(8,128)(2,1)S(1)} %shard_map.119.refs_7_), channel_id=1, source_target_pairs={{4,0},{0,4},{12,8},{8,12},{5,1},{1,5},{13,9},{9,13},{6,2},{2,6},{1... | collective-permute-start | bytes 884744 | tf_op jit(solution)/shard_map/ppermute | solution.py:299
  8.9 7.2 %collective-permute-start.3 = (bf16[144,256]{1,0:T(8,128)(2,1)S(1)}, bf16[144,256]{1,0:T(8,128)(2,1)S(1)}, u32[]{:S(2)}, u32[]{:S(2)}) collective-permute-start(bf16[144,256]{1,0:T(8,128)(2,1)S(1)} %shard_map.118.refs_1_), channel_id=1, source_target_pairs={{8,0},{12,4},{0,8},{4,12},{9,1},{13,5},{1,9},{5,13},{10,2},{14,6},... | collective-permute-start | bytes 221192 | tf_op jit(solution)/shard_map/ppermute | solution.py:200
  16.0 4.4 %collective-permute-start.4 = (bf16[144,256]{1,0:T(8,128)(2,1)S(1)}, bf16[144,256]{1,0:T(8,128)(2,1)S(1)}, u32[]{:S(2)}, u32[]{:S(2)}) collective-permute-start(bf16[144,256]{1,0:T(8,128)(2,1)S(1)} %collective-permute-done.3.refs_0_), channel_id=1, source_target_pairs={{2,0},{0,2},{3,1},{1,3},{6,4},{4,6},{7,5},{5,7},{10,8},{8,10},{11,... | collective-permute-start | bytes 221192 | tf_op jit(solution)/shard_map/ppermute | solution.py:195
  17.5 4.4 %collective-permute-start = (bf16[144,256]{1,0:T(8,128)(2,1)S(1)}, bf16[144,256]{1,0:T(8,128)(2,1)S(1)}, u32[]{:S(2)}, u32[]{:S(2)}) collective-permute-start(bf16[144,256]{1,0:T(8,128)(2,1)S(1)} %shard_map.118.refs_1_), channel_id=1, source_target_pairs={{2,0},{0,2},{3,1},{1,3},{6,4},{4,6},{7,5},{5,7},{10,8},{8,10},{11,... | collective-permute-start | bytes 221192 | tf_op jit(solution)/shard_map/ppermute | solution.py:195
  18.0 3.8 %collective-permute-start.5 = (bf16[144,256]{1,0:T(8,128)(2,1)S(1)}, bf16[144,256]{1,0:T(8,128)(2,1)S(1)}, u32[]{:S(2)}, u32[]{:S(2)}) collective-permute-start(bf16[144,256]{1,0:T(8,128)(2,1)S(1)} %collective-permute-done.3.refs_0_), channel_id=1, source_target_pairs={{1,0},{0,1},{3,2},{2,3},{5,4},{4,5},{7,6},{6,7},{9,8},{8,9},{11,10... | collective-permute-start | bytes 221192 | tf_op jit(solution)/shard_map/ppermute | solution.py:195
  20.4 1.5 %collective-permute-start.6 = (bf16[144,256]{1,0:T(8,128)(2,1)S(1)}, bf16[144,256]{1,0:T(8,128)(2,1)S(1)}, u32[]{:S(2)}, u32[]{:S(2)}) collective-permute-start(bf16[144,256]{1,0:T(8,128)(2,1)S(1)} %collective-permute-done.4.refs_1_), channel_id=1, source_target_pairs={{1,0},{0,1},{3,2},{2,3},{5,4},{4,5},{7,6},{6,7},{9,8},{8,9},{11,10... | collective-permute-start | bytes 221192 | tf_op jit(solution)/shard_map/ppermute | solution.py:195
  21.9 6.8 %collective-permute-start.1 = (bf16[144,256]{1,0:T(8,128)(2,1)S(1)}, bf16[144,256]{1,0:T(8,128)(2,1)S(1)}, u32[]{:S(2)}, u32[]{:S(2)}) collective-permute-start(bf16[144,256]{1,0:T(8,128)(2,1)S(1)} %collective-permute-done.refs_2_), channel_id=1, source_target_pairs={{1,0},{0,1},{3,2},{2,3},{5,4},{4,5},{7,6},{6,7},{9,8},{8,9},{11,10... | collective-permute-start | bytes 221192 | tf_op jit(solution)/shard_map/ppermute | solution.py:195
  23.6 8.2 %collective-permute-start.7 = (bf16[64,384]{1,0:T(8,128)(2,1)S(1)}, bf16[64,384]{1,0:T(8,128)(2,1)S(1)}, u32[]{:S(2)}, u32[]{:S(2)}) collective-permute-start(bf16[64,384]{1,0:T(8,128)(2,1)S(1)} %get-tuple-element.17), channel_id=1, source_target_pairs={{8,0},{12,4},{0,8},{4,12},{9,1},{13,5},{1,9},{5,13},{10,2},{14,6},... | collective-permute-start | bytes 147464 | tf_op jit(solution)/shard_map/ppermute | solution.py:200
  28.5 5.7 %collective-permute-start.8 = (bf16[64,384]{1,0:T(8,128)(2,1)S(1)}, bf16[64,384]{1,0:T(8,128)(2,1)S(1)}, u32[]{:S(2)}, u32[]{:S(2)}) collective-permute-start(bf16[64,384]{1,0:T(8,128)(2,1)S(1)} %shard_map.123), channel_id=1, source_target_pairs={{8,0},{12,4},{0,8},{4,12},{9,1},{13,5},{1,9},{5,13},{10,2},{14,6},... | collective-permute-start | bytes 147464 | tf_op jit(solution)/shard_map/ppermute | solution.py:200

commit v3 on v2

--- a/solution.py
+++ b/solution.py
@@ -8,14 +8,16 @@
 from jax.experimental.pallas import tpu as pltpu
 from jax.sharding import PartitionSpec as P
 
+
 REACH = 4
 WIN = 2 * REACH + 1
 LENGTH_ROWS = 16
+KERNEL_BYTES = 16 << 20
 BF16 = jnp.bfloat16
 F32 = jnp.float32
 VMEM = pl.BlockSpec(memory_space=pltpu.VMEM)
 SMEM = pl.BlockSpec(memory_space=pltpu.SMEM)
-ANY = pl.BlockSpec(memory_space=pl.ANY)
+HBM = pl.BlockSpec(memory_space=pltpu.HBM)
 
 
 def near(array):
@@ -31,35 +33,63 @@
         in_specs=in_specs,
         out_specs=out_specs,
         scratch_shapes=list(scratch),
+        compiler_params=pltpu.CompilerParams(vmem_limit_bytes=KERNEL_BYTES),
         cost_estimate=pl.CostEstimate(flops=flops, bytes_accessed=moved, transcendentals=0),
     )(*args)
 
 
-def pack_kernel(lengths_ref, history_ref, piece_ref):
-    rows, width = piece_ref.shape
-    tokens = history_ref.shape[1]
-    users = (rows - LENGTH_ROWS) // tokens
+def prepare_kernel(shares, *refs):
+    sources, outs, scratch = refs[:9], refs[9:13], refs[13:]
+    history_ref, sources = sources[0], sources[1:]
+    piece_ref, items_out, heads_ref, bias_out = outs
+    held, sems, token_sem = scratch[:8], scratch[8], scratch[9]
+    copies = [pltpu.make_async_copy(*pair, sems.at[i]) for i, pair in enumerate(zip(sources, held))]
+    users, tokens, _ = history_ref.shape
+    users //= shares
     first = lax.axis_index("sub") * users
-    piece_ref[: users * tokens, :] = history_ref[pl.ds(first, users)].reshape(users * tokens, width)
+    width = piece_ref.shape[1]
+    moves = []
+    for user in range(users):
+        place = piece_ref.at[pl.ds(user * tokens, tokens)]
+        moves.append(pltpu.make_async_copy(history_ref.at[first + user], place, token_sem.at[user]))
+    for copy in copies + moves:
+        copy.start()
+    rows_ref, w_query_ref, w_item_ref, w_joint_ref, bias_ref, w_task_ref, bias_task_ref, lengths_ref = held
+
+    for copy in copies[5:]:
+        copy.wait()
     row = lax.broadcasted_iota(jnp.int32, (LENGTH_ROWS, width), 0)
     lengths = jnp.zeros((LENGTH_ROWS, width), F32)
     for user in range(users):
         lengths = jnp.where(row == user, lengths_ref[first + user].astype(F32), lengths)
     piece_ref[users * tokens :, :] = lengths.astype(BF16)
-
-
-def project_kernel(items_ref, w_query_ref, w_item_ref, w_joint_ref, bias_ref, out_ref):
-    width = w_query_ref.shape[1]
-    rows = items_ref[...]
+    tasks, hid = w_task_ref.shape
+    w_task = w_task_ref[...].astype(F32)
+    blank = jnp.zeros_like(w_task)
+    heads_ref[:, :hid] = jnp.concatenate([w_task, blank], 0).astype(BF16)
+    heads_ref[:, hid:] = jnp.concatenate([blank, w_task], 0).astype(BF16)
+    row = lax.broadcasted_iota(jnp.int32, bias_out.shape, 0) % tasks
+    bias = jnp.zeros(bias_out.shape, F32)
+    for task in range(tasks):
+        bias = jnp.where(row == task, bias_task_ref[task], bias)
+    bias_out[...] = bias
+
+    for copy in copies[:5]:
+        copy.wait()
+    rows = rows_ref[...]
     queries = jnp.dot(rows, w_query_ref[...], preferred_element_type=F32)
-    out_ref[:width, :] = queries.T.astype(BF16)
+    items_out[:width, :] = queries.T.astype(BF16)
     joined = jnp.dot(rows, w_item_ref[...], preferred_element_type=F32).astype(BF16)
     terms = jnp.dot(joined, w_joint_ref[...], preferred_element_type=F32) + bias_ref[...]
-    out_ref[width:, :] = terms.T.astype(BF16)
+    items_out[width:, :] = terms.T.astype(BF16)
+    for move in moves:
+        move.wait()
 
 
 def keys_values(pieces, turn, w_key_ref, w_value_ref, w_pooled_ref, key_ref, pooled_ref, mask_ref, history_ref):
-    pairs, _, both = pooled_ref.shape
+    pairs, hid, depth = pooled_ref.shape
+    hid //= 2
+    both = depth - hid
     full = both // 2
     users = 2 * pairs
     share = users // len(pieces)
@@ -75,33 +105,27 @@
     key_ref[...] = jnp.dot(history_ref[...], w_key_ref[...], preferred_element_type=F32).astype(BF16)
     values = jnp.dot(history_ref[...], w_value_ref[...], preferred_element_type=F32).astype(BF16)
     pooled = jnp.dot(values, w_pooled_ref[...], preferred_element_type=F32)
-    hid = pooled.shape[1]
     lane = lax.broadcasted_iota(jnp.int32, (hid, both), 1)
+    one = lax.broadcasted_iota(jnp.int32, (2 * hid, hid), 0) % hid
+    one = jnp.where(one == lax.broadcasted_iota(jnp.int32, (2 * hid, hid), 1), 1.0, 0.0).astype(BF16)
     for pair in range(pairs):
         flat = pooled[pair * both : (pair + 1) * both].T
-        pooled_ref[pair, :hid, :] = jnp.where(lane < full, flat, 0.0).astype(BF16)
-        pooled_ref[pair, hid:, :] = jnp.where(lane < full, 0.0, flat).astype(BF16)
-
-
-def score(items_ref, state, w_task_ref, bias_task_ref, out_ref, scratch, shares):
+        pooled_ref[pair, :hid, :both] = jnp.where(lane < full, flat, 0.0).astype(BF16)
+        pooled_ref[pair, hid:, :both] = jnp.where(lane < full, 0.0, flat).astype(BF16)
+        pooled_ref[pair, :, both:] = one
+
+
+def score(items_ref, state, heads_ref, bias_ref, out_ref, scratch, shares):
     key_ref, pooled_ref, mask_ref = state
     scores_ref, weights_ref, hidden_ref = scratch
     width = key_ref.shape[1]
-    tasks, hid = w_task_ref.shape
-    pairs, _, both = pooled_ref.shape
+    tasks = heads_ref.shape[0] // 2
+    pairs, hid, depth = pooled_ref.shape
+    both = depth - hid // 2
     full = both // 2
     share = pairs // shares
     columns = items_ref.shape[1]
     factor = math.log2(math.e) / math.sqrt(width)
-    w_task = w_task_ref[...].astype(F32)
-    blank = jnp.zeros_like(w_task)
-    heads = jnp.concatenate(
-        [jnp.concatenate([w_task, blank], 1), jnp.concatenate([blank, w_task], 1)], 0
-    ).astype(BF16)
-    row = lax.broadcasted_iota(jnp.int32, (2 * tasks, columns), 0)
-    bias = jnp.zeros((2 * tasks, columns), F32)
-    for task in range(tasks):
-        bias = jnp.where(row % tasks == task, bias_task_ref[task], bias)
 
     scores_ref[...] = jnp.dot(key_ref[...], items_ref[:width, :], preferred_element_type=F32)
     for user in range(2 * pairs):
@@ -115,13 +139,12 @@
             weights_ref[rows, lanes] = weights.astype(BF16)
     for pair in range(pairs):
         rows = slice(pair * both, (pair + 1) * both)
-        total = jnp.dot(pooled_ref[pair], weights_ref[rows, :], preferred_element_type=F32)
-        for user in range(2):
-            part = slice(user * hid, (user + 1) * hid)
-            hidden = total[part] + items_ref[width:, :].astype(F32)
-            hidden_ref[pair, part, :] = jnp.maximum(hidden, 0.0).astype(BF16)
+        inputs = jnp.concatenate([weights_ref[rows, :], items_ref[width:, :]], 0)
+        hidden = jnp.dot(pooled_ref[pair], inputs, preferred_element_type=F32)
+        hidden_ref[pair] = jnp.maximum(hidden, 0.0).astype(BF16)
+    bias = jnp.concatenate([bias_ref[...]] * (columns // 128), 1)
     for pair in range(pairs):
-        logits = jnp.dot(heads, hidden_ref[pair], preferred_element_type=F32) + bias
+        logits = jnp.dot(heads_ref[...], hidden_ref[pair], preferred_element_type=F32) + bias
         first = lax.rem(lax.axis_index("sub") + pair // share, shares) * share + pair % share
         if len(out_ref.shape) == 3:
             out_ref[2 * first] = logits[:tasks]
@@ -138,12 +161,12 @@
     count = given.count(False)
     sent, refs = list(refs[:count]), refs[count:]
     piece_refs = [None if local else sent.pop(0) for local in given]
-    w_key_ref, w_value_ref, w_pooled_ref, items_ref, w_task_ref, bias_task_ref = refs[:6]
+    w_key_ref, w_value_ref, w_pooled_ref, items_ref, heads_ref, bias_ref = refs[:6]
     out_ref, key_ref, pooled_ref, mask_ref, rows_ref, *scratch = refs[6:]
     me, side = lax.axis_index("users"), lax.axis_index("sub")
     pieces, turn = [], []
     rows = piece_refs[0].shape[0] - LENGTH_ROWS
-    tokens = pooled_ref.shape[2] // 2 // parts
+    tokens = (pooled_ref.shape[2] - pooled_ref.shape[1] // 2) // 2 // parts
     for s in range(shares):
         entries = []
         for r in range(parts):
@@ -159,12 +182,12 @@
         turn.append(piece_refs[s * parts + parts - 1][rows:, :].astype(F32))
     state = (key_ref, pooled_ref, mask_ref)
     keys_values(pieces, turn, w_key_ref, w_value_ref, w_pooled_ref, *state, rows_ref)
-    score(items_ref, state, w_task_ref, bias_task_ref, out_ref, scratch, shares)
-
-
-def next_kernel(shares, items_ref, key_ref, pooled_ref, mask_ref, w_task_ref, bias_task_ref, out_ref, *scratch):
+    score(items_ref, state, heads_ref, bias_ref, out_ref, scratch, shares)
+
+
+def next_kernel(shares, items_ref, key_ref, pooled_ref, mask_ref, heads_ref, bias_ref, out_ref, *scratch):
     state = (key_ref, pooled_ref, mask_ref)
-    score(items_ref, state, w_task_ref, bias_task_ref, out_ref, scratch, shares)
+    score(items_ref, state, heads_ref, bias_ref, out_ref, scratch, shares)
 
 
 def place_kernel(count, *refs):
@@ -201,11 +224,17 @@
 
 
 def spread(piece, shares, parts, own=False):
-    row = [piece] + [shift(piece, "users", r) for r in range(1, parts)]
+    row = [piece]
+    for r in range(1, parts):
+        row.append(shift(piece, "users", r))
     table = [row]
     for s in range(1, shares):
-        away = [shift(entry, "sub", s) for entry in row[1:]]
-        table.append([None if own and parts > 1 else shift(piece, "sub", s)] + away)
+        line = [None]
+        for r in range(parts):
+            if r or not own or parts == 1:
+                entry = shift(row[r], "sub", s)
+                line[r:] = [entry]
+        table.append(line)
     return table
 
 
@@ -229,26 +258,31 @@
     count, parts, shares = (lax.axis_size(axis) for axis in ("blk", "users", "sub"))
     full = tokens * parts
 
-    piece = call(
-        pack_kernel,
-        pltpu.VMEM((users // shares * tokens + LENGTH_ROWS, width), BF16),
-        [SMEM, VMEM],
-        VMEM,
-        (lengths, history),
-        0,
-    )
-    mine = call(
-        project_kernel,
-        pltpu.VMEM((width + hid, items), BF16),
-        [VMEM] * 5,
-        VMEM,
-        (item_rows, w_query, w_item, w_joint, bias_hidden[None]),
+    sources = (item_rows, w_query, w_item, w_joint, bias_hidden[None], w_task.T)
+    piece, mine, heads, bias = call(
+        functools.partial(prepare_kernel, shares),
+        (
+            pltpu.VMEM((users // shares * tokens + LENGTH_ROWS, width), BF16),
+            pltpu.VMEM((width + hid, items), BF16),
+            pltpu.VMEM((2 * tasks, 2 * hid), BF16),
+            pltpu.VMEM((2 * tasks, 128), F32),
+        ),
+        [HBM] * 9,
+        [VMEM] * 4,
+        (history, *sources, bias_task, lengths),
         2 * items * item_rows.shape[1] * 2 * width,
+        (
+            *(pltpu.VMEM(a.shape, a.dtype) for a in sources),
+            pltpu.SMEM(bias_task.shape, F32),
+            pltpu.SMEM(lengths.shape, jnp.int32),
+            pltpu.SemaphoreType.DMA((8,)),
+            pltpu.SemaphoreType.DMA((users // shares,)),
+        ),
     )
     flops = 2 * users * items * (full * (width + hid) + hid * tasks)
     state = (
         pltpu.VMEM((users * full, width), BF16),
-        pltpu.VMEM((users // 2, 2 * hid, 2 * full), BF16),
+        pltpu.VMEM((users // 2, 2 * hid, 2 * full + hid), BF16),
         pltpu.VMEM((users * full, 128), F32),
     )
     kept = pltpu.VMEM((users, tasks, items), F32)
@@ -265,9 +299,9 @@
         result = call(
             functools.partial(first_kernel, own, shares, parts),
             (out, *state),
-            [VMEM] * (len(head) + len(flat) + 5) + [SMEM],
+            [VMEM] * (len(head) + len(flat) + 6),
             [VMEM] * 4,
-            (*head, *flat, w_key, w_value, w_pooled, block, w_task.T, bias_task),
+            (*head, *flat, w_key, w_value, w_pooled, block, heads, bias),
             flops + 4 * users * full * width * width,
             (pltpu.VMEM((users * full, width), BF16), *scratch),
         )
@@ -277,16 +311,17 @@
         return call(
             functools.partial(next_kernel, shares),
             out,
-            [VMEM] * 5 + [SMEM],
+            [VMEM] * 6,
             VMEM,
-            (block, *held, w_task.T, bias_task),
+            (block, *held, heads, bias),
             flops,
             scratch,
         )
 
     if count % 2 or count > WIN:
         window = [None] * WIN
-        window[REACH], held = start(spread(piece, shares, parts, True), mine, kept, True)
+        table = spread(piece, shares, parts, True)
+        window[REACH], held = start(table, mine, kept, True)
         low = high = mine
         for offset in range(1, REACH + 1):
             low, high = shift(low, "blk", -1), shift(high, "blk", 1)
@@ -294,15 +329,19 @@
             window[REACH + offset] = go_on(held, high, kept)
         return jnp.stack(window, axis=1)
 
-    far = [from_pair(piece, ahead) for ahead in range(1, count // 2)]
+    far = []
+    for ahead in range(1, count // 2):
+        far.append(from_pair(piece, ahead))
+    other = lax.ppermute(mine, "blk", [(i ^ 1, i) for i in range(count)])
     own = spread(piece, shares, parts, True)
-    other = lax.ppermute(mine, "blk", [(i ^ 1, i) for i in range(count)])
     at_home, held = start(own, mine, kept, True)
     away = []
     for ahead, entry in enumerate(far, 1):
-        result, guests = start(spread(entry, shares, parts), mine, sent, False)
+        table = spread(entry, shares, parts)
+        result, guests = start(table, mine, sent, False)
         back = [from_pair(result, -ahead)]
-        back.append(from_pair(go_on(guests, other, sent), -ahead))
+        result = go_on(guests, other, sent)
+        back.append(from_pair(result, -ahead))
         away.append(back)
     beside = go_on(held, other, kept)
     results = [entry for back in reversed(away) for entry in back]
@@ -310,7 +349,7 @@
         functools.partial(place_kernel, count),
         jax.ShapeDtypeStruct((users, WIN, tasks, items), F32),
         [VMEM] * count,
-        ANY,
+        HBM,
         (at_home, beside, *results),
         0,
         (pltpu.VMEM((count, users, tasks, items), F32), pltpu.SemaphoreType.DMA((WIN,))),
@@ -332,6 +371,7 @@
         P(),
         P(),
     )
+
     return jax.shard_map(
         shards,
         mesh=mesh,

time: 35.6 us -> 36.4 us (1.022)
  waiting for transfers between devices: 10.8 us -> 12.8 us
  Pallas kernels: 8.72 us -> 6.73 us
  local copies, waits for them, and re-layouts: 4.41 us -> 5.35 us
    ppermute x3, waiting for transfers between devices: 6.94 us -> 8.97 us  [from_pair(): lax.ppermute(block, 'blk', [((i + 2 * distance) % count, i) for i in rang...]
    pallas_call x7 -> x6, Pallas kernels: 8.72 us -> 6.73 us  [call(): pl.pallas_call(kernel, out_shape=out_shape, in_specs=in_specs, out_specs=...]
    unnamed x20 -> x26, local copies, waits for them, and re-layouts: 4.41 us -> 5.35 us
  transfers between devices with their start and end apart: 9 -> 9, of which waited for: 4 -> 4; matrix products, arithmetic and copies ran while one was open for 0% -> 0% of each run, Pallas kernels for 20% -> 11%
where the time goes in v3:
time: 36.4 us; the launch traced here: 36.1 us
  waiting for transfers between devices  12.8 us (35%)
  starting transfers between devices  11.2 us (31%)
  Pallas kernels  6.73 us (18%)
  local copies, waits for them, and re-layouts  5.35 us (15%)
    ppermute x3, waiting for transfers between devices, from_pair(): lax.ppermute(block, 'blk', [((i + 2 * distance) % count, i) for i in rang...  8.97 us
    pallas_call x6, Pallas kernels, call(): pl.pallas_call(kernel, out_shape=out_shape, in_specs=in_specs, out_specs=...  6.73 us
    ppermute x3, starting transfers between devices, from_pair(): lax.ppermute(block, 'blk', [((i + 2 * distance) % count, i) for i in rang...  6.01 us
    unnamed x26, local copies, waits for them, and re-layouts  5.35 us
    ppermute x5, waiting for transfers between devices, shift(): lax.ppermute(block, axis, [((i + distance) % count, i) for i in range(cou...  3.82 us
    ppermute x1, starting transfers between devices, shards(): other = lax.ppermute(mine, 'blk', [(i ^ 1, i) for i in range(count)])  3.12 us
    ppermute x5, starting transfers between devices, shift(): lax.ppermute(block, axis, [((i + distance) % count, i) for i in range(cou...  2.03 us
  transfers between devices with their start and end apart: 9, of which 4 were waited for; matrix products, arithmetic and copies ran while one was open for 0% of the time, Pallas kernels for 11%

profile of v3, /device:TPU:0, one launch (start us, length us, event | category | flops | bytes accessed | tf_op | source)
XLA Modules:
  0.0 36.1 jit_solution(4029210478167507254)
XLA Ops:
  0.0 0.0 copy-start.6
  0.0 0.0 copy-start.7
  0.0 0.0 copy-start.8
  0.0 0.0 copy-start.9
  0.0 0.7 %copy-done.6 = bf16[128,8]{0,1:T(8,128)(2,1)S(1)} copy-done((bf16[128,8]{0,1:T(8,128)(2,1)S(1)}, bf16[128,8]{0,1:T(8,128)(2,1)}, u32[]{:S(2)}) %copy-start.6) | copy-done | bytes 2072
  0.7 0.0 copy-done.7
  0.7 0.0 copy-done.8
  0.7 0.0 copy-done.9
  0.7 0.0 copy-start
  0.7 1.0 %copy-done = bf16[384,512]{1,0:T(8,128)(2,1)S(1)} copy-done((bf16[384,512]{1,0:T(8,128)(2,1)S(1)}, bf16[384,512]{1,0:T(8,128)(2,1)}, u32[]{:S(2)}) %copy-start) | copy-done | bytes 393240
  1.7 0.0 copy-start.1
  1.7 0.9 %copy-done.1 = bf16[512,256]{1,0:T(8,128)(2,1)S(1)} copy-done((bf16[512,256]{1,0:T(8,128)(2,1)S(1)}, bf16[512,256]{1,0:T(8,128)(2,1)}, u32[]{:S(2)}) %copy-start.1) | copy-done | bytes 262168
  2.7 0.0 copy-start.2
  2.7 0.9 %copy-done.2 = bf16[512,256]{1,0:T(8,128)(2,1)S(1)} copy-done((bf16[512,256]{1,0:T(8,128)(2,1)S(1)}, bf16[512,256]{1,0:T(8,128)(2,1)}, u32[]{:S(2)}) %copy-start.2) | copy-done | bytes 262168
  3.6 0.0 copy-start.3
  3.6 0.9 %copy-done.3 = bf16[8,32,256]{2,1,0:T(8,128)(2,1)S(1)} copy-done((bf16[8,32,256]{2,1,0:T(8,128)(2,1)S(1)}, bf16[8,32,256]{2,1,0:T(8,128)(2,1)}, u32[]{:S(2)}) %copy-start.3) | copy-done | bytes 131096
  4.5 0.0 copy-start.5
  4.5 0.8 %copy-done.5 = bf16[256,128]{1,0:T(8,128)(2,1)S(1)} copy-done((bf16[256,128]{1,0:T(8,128)(2,1)S(1)}, bf16[256,128]{1,0:T(8,128)(2,1)}, u32[]{:S(2)}) %copy-start.5) | copy-done | bytes 65560
  5.3 0.0 copy-start.10
  5.3 0.0 copy-start.11
  5.3 0.0 copy-start.12
  5.4 1.6 %shard_map.118 = (bf16[144,256]{1,0:T(8,128)(2,1)S(1)}, bf16[384,384]{1,0:T(8,128)(2,1)S(1)}, bf16[16,256]{1,0:T(8,128)(2,1)S(1)}, f32[16,128]{1,0:T(8,128)S(1)}) custom-call(bf16[8,32,256]{2,1,0:T(8,128)(2,1)S(1)} %copy-done.3, bf16[384,512]{1,0:T(8,128)(2,1)S(1)} %copy-done, bf16[512,256]{1,0:T(8,128)(2,1)S(1)} %copy-done.1, ...), custom_call_target="tpu_custom_call" | custom-call | flops 201326592 | bytes 1116736 | tf_op jit(solution)/shard_map/pallas_call | solution.py:30
  7.0 3.1 %collective-permute-start.2 = (bf16[384,384]{1,0:T(8,128)(2,1)S(1)}, bf16[384,384]{1,0:T(8,128)(2,1)S(1)}, u32[]{:S(2)}, u32[]{:S(2)}) collective-permute-start(bf16[384,384]{1,0:T(8,128)(2,1)S(1)} %get-tuple-element.18.refs_7_), channel_id=1, source_target_pairs={{4,0},{0,4},{12,8},{8,12},{5,1},{1,5},{13,9},{9,13},{6,2},{2,6},{1... | collective-permute-start | bytes 884744 | tf_op jit(solution)/shard_map/ppermute | solution.py:335
  10.1 2.6 %collective-permute-start.3 = (bf16[144,256]{1,0:T(8,128)(2,1)S(1)}, bf16[144,256]{1,0:T(8,128)(2,1)S(1)}, u32[]{:S(2)}, u32[]{:S(2)}) collective-permute-start(bf16[144,256]{1,0:T(8,128)(2,1)S(1)} %get-tuple-element.17.refs_1_), channel_id=1, source_target_pairs={{8,0},{12,4},{0,8},{4,12},{9,1},{13,5},{1,9},{5,13},{10,2},{14,6},... | collective-permute-start | bytes 221192 | tf_op jit(solution)/shard_map/ppermute | solution.py:223
  12.7 5.3 %collective-permute-done.3.refs_0_ = bf16[144,256]{1,0:T(8,128)(2,1)S(1)} collective-permute-done((bf16[144,256]{1,0:T(8,128)(2,1)S(1)}, bf16[144,256]{1,0:T(8,128)(2,1)S(1)}, u32[]{:S(2)}, u32[]{:S(2)}) %collective-permute-start.3) | collective-permute-done | bytes 73760 | tf_op jit(solution)/shard_map/ppermute | solution.py:223
  17.9 1.5 %collective-permute-start.4 = (bf16[144,256]{1,0:T(8,128)(2,1)S(1)}, bf16[144,256]{1,0:T(8,128)(2,1)S(1)}, u32[]{:S(2)}, u32[]{:S(2)}) collective-permute-start(bf16[144,256]{1,0:T(8,128)(2,1)S(1)} %collective-permute-done.3.refs_0_), channel_id=1, source_target_pairs={{2,0},{0,2},{3,1},{1,3},{6,4},{4,6},{7,5},{5,7},{10,8},{8,10},{11,... | collective-permute-start | bytes 221192 | tf_op jit(solution)/shard_map/ppermute | solution.py:218
  19.4 0.5 %collective-permute-start = (bf16[144,256]{1,0:T(8,128)(2,1)S(1)}, bf16[144,256]{1,0:T(8,128)(2,1)S(1)}, u32[]{:S(2)}, u32[]{:S(2)}) collective-permute-start(bf16[144,256]{1,0:T(8,128)(2,1)S(1)} %get-tuple-element.17.refs_1_), channel_id=1, source_target_pairs={{2,0},{0,2},{3,1},{1,3},{6,4},{4,6},{7,5},{5,7},{10,8},{8,10},{11,... | collective-permute-start | bytes 221192 | tf_op jit(solution)/shard_map/ppermute | solution.py:218
  20.0 0.0 collective-permute-start.5
  20.0 2.3 %collective-permute-done.4.refs_1_ = bf16[144,256]{1,0:T(8,128)(2,1)S(1)} collective-permute-done((bf16[144,256]{1,0:T(8,128)(2,1)S(1)}, bf16[144,256]{1,0:T(8,128)(2,1)S(1)}, u32[]{:S(2)}, u32[]{:S(2)}) %collective-permute-start.4) | collective-permute-done | bytes 73760 | tf_op jit(solution)/shard_map/ppermute | solution.py:218
  22.3 0.0 collective-permute-start.6
  22.3 1.5 %collective-permute-done.refs_2_ = bf16[144,256]{1,0:T(8,128)(2,1)S(1)} collective-permute-done((bf16[144,256]{1,0:T(8,128)(2,1)S(1)}, bf16[144,256]{1,0:T(8,128)(2,1)S(1)}, u32[]{:S(2)}, u32[]{:S(2)}) %collective-permute-start) | collective-permute-done | bytes 73760 | tf_op jit(solution)/shard_map/ppermute | solution.py:218
  23.8 0.0 collective-permute-start.1
  23.8 0.0 collective-permute-done.5.refs_2_
  23.8 0.0 collective-permute-done.6.refs_3_
  23.8 0.0 copy-done.10
  23.8 0.0 copy-done.11
  23.8 0.0 copy-done.12
  23.8 1.2 %shard_map.121 = (bf16[64,384]{1,0:T(8,128)(2,1)S(1)}, bf16[512,256]{1,0:T(8,128)(2,1)S(1)}, bf16[4,256,256]{2,1,0:T(8,128)(2,1)S(1)}, f32[512,128]{1,0:T(8,128)S(1)}) custom-call(bf16[144,256]{1,0:T(8,128)(2,1)S(1)} %collective-permute-done.3.refs_0_, bf16[144,256]{1,0:T(8,128)(2,1)S(1)} %collective-permute-done.4.refs_1_, ...), custom_call_target="tpu_custom_call" | custom-call | flops 291504128 | bytes 933888 | tf_op jit(solution)/shard_map/pallas_call | solution.py:30
  25.0 3.4 %collective-permute-start.7 = (bf16[64,384]{1,0:T(8,128)(2,1)S(1)}, bf16[64,384]{1,0:T(8,128)(2,1)S(1)}, u32[]{:S(2)}, u32[]{:S(2)}) collective-permute-start(bf16[64,384]{1,0:T(8,128)(2,1)S(1)} %get-tuple-element.25), channel_id=1, source_target_pairs={{8,0},{12,4},{0,8},{4,12},{9,1},{13,5},{1,9},{5,13},{10,2},{14,6},... | collective-permute-start | bytes 147464 | tf_op jit(solution)/shard_map/ppermute | solution.py:223
  28.4 0.0 collective-permute-done.2.items_ref
  28.4 0.0 copy-start.4
  28.4 0.9 %shard_map.122 = bf16[64,384]{1,0:T(8,128)(2,1)S(1)} custom-call(bf16[384,384]{1,0:T(8,128)(2,1)S(1)} %collective-permute-done.2.items_ref, bf16[512,256]{1,0:T(8,128)(2,1)S(1)} %get-tuple-element.26.key_ref, bf16[4,256,256]{2,1,0:T(8,128)(2,1)S(1)} %get-tuple-element.27.pooled_ref, f32[512,128]{1,0:T(8,128)S(1)} %get-tuple-element.28.mask_ref, ...), custom_call_target="tpu_custom_call" | custom-call | flops 157286400 | bytes 1359872 | tf_op jit(solution)/shard_map/pallas_call | solution.py:30
  29.3 0.0 collective-permute-start.8
  29.3 0.0 collective-permute-done.1.refs_3_
  29.3 0.0 copy-done.4
  29.3 1.2 %shard_map.119 = (f32[8,8,384]{2,1,0:T(8,128)S(1)}, bf16[512,256]{1,0:T(8,128)(2,1)S(1)}, bf16[4,256,256]{2,1,0:T(8,128)(2,1)S(1)}, f32[512,128]{1,0:T(8,128)S(1)}) custom-call(bf16[8,32,256]{2,1,0:T(8,128)(2,1)S(1)} %copy-done.4, bf16[144,256]{1,0:T(8,128)(2,1)S(1)} %get-tuple-element.17.refs_1_, bf16[144,256]{1,0:T(8,128)(2,1)S(1)} %collective-permute-done.refs_2_, ...), custom_call_target="tpu_custom_call" | custom-call | flops 291504128 | bytes 991232 | tf_op jit(solution)/shard_map/pallas_call | solution.py:30
  30.5 0.9 %shard_map.120.refs_1_ = f32[8,8,384]{2,1,0:T(8,128)S(1)} custom-call(bf16[384,384]{1,0:T(8,128)(2,1)S(1)} %collective-permute-done.2.items_ref, bf16[512,256]{1,0:T(8,128)(2,1)S(1)} %get-tuple-element.22.key_ref, bf16[4,256,256]{2,1,0:T(8,128)(2,1)S(1)} %get-tuple-element.23.pooled_ref, f32[512,128]{1,0:T(8,128)S(1)} %get-tuple-element.24.mask_ref, ...), custom_call_target="tpu_custom_call" | custom-call | flops 157286400 | bytes 1359872 | tf_op jit(solution)/shard_map/pallas_call | solution.py:30
  31.4 0.0 collective-permute-done.7.refs_2_
  31.4 3.7 %collective-permute-done.8.refs_3_ = bf16[64,384]{1,0:T(8,128)(2,1)S(1)} collective-permute-done((bf16[64,384]{1,0:T(8,128)(2,1)S(1)}, bf16[64,384]{1,0:T(8,128)(2,1)S(1)}, u32[]{:S(2)}, u32[]{:S(2)}) %collective-permute-start.8) | collective-permute-done | bytes 49184 | tf_op jit(solution)/shard_map/ppermute | solution.py:223
  35.1 1.0 %shard_map.123 = f32[8,9,8,384]{3,2,1,0:T(8,128)} custom-call(f32[8,8,384]{2,1,0:T(8,128)S(1)} %get-tuple-element.21.refs_0_, f32[8,8,384]{2,1,0:T(8,128)S(1)} %shard_map.120.refs_1_, bf16[64,384]{1,0:T(8,128)(2,1)S(1)} %collective-permute-done.7.refs_2_, bf16[64,384]{1,0:T(8,128)(2,1)S(1)} %collective-permute-done.8.refs_3_), custom_call_target="tpu_custom_call" | custom-call | bytes 294912 | tf_op jit(solution)/shard_map/pallas_call | solution.py:30
Async XLA Ops:
  0.0 0.7 %copy-start.6 = (bf16[128,8]{0,1:T(8,128)(2,1)S(1)}, bf16[128,8]{0,1:T(8,128)(2,1)}, u32[]{:S(2)}) copy-start(bf16[128,8]{0,1:T(8,128)(2,1)} %param.22) | copy-start | bytes 6148
  0.0 0.7 %copy-start.7 = (f32[128]{0:T(128)S(1)}, f32[128]{0:T(128)}, u32[]{:S(2)}) copy-start(f32[128]{0:T(128)} %param.21) | copy-start | bytes 1540
  0.0 0.7 %copy-start.8 = (f32[8]{0:T(128)S(1)}, f32[8]{0:T(128)}, u32[]{:S(2)}) copy-start(f32[8]{0:T(128)} %refs_7_.1) | copy-start | bytes 100
  0.0 0.7 %copy-start.9 = (s32[8]{0:T(128)S(1)}, s32[8]{0:T(128)}, u32[]{:S(2)}) copy-start(s32[8]{0:T(128)} %refs_8_.1) | copy-start | bytes 100
  0.7 1.0 %copy-start = (bf16[384,512]{1,0:T(8,128)(2,1)S(1)}, bf16[384,512]{1,0:T(8,128)(2,1)}, u32[]{:S(2)}) copy-start(bf16[384,512]{1,0:T(8,128)(2,1)} %refs_1_.1) | copy-start | bytes 1179652
  1.7 0.9 %copy-start.1 = (bf16[512,256]{1,0:T(8,128)(2,1)S(1)}, bf16[512,256]{1,0:T(8,128)(2,1)}, u32[]{:S(2)}) copy-start(bf16[512,256]{1,0:T(8,128)(2,1)} %refs_2_.1) | copy-start | bytes 786436
  2.7 0.9 %copy-start.2 = (bf16[512,256]{1,0:T(8,128)(2,1)S(1)}, bf16[512,256]{1,0:T(8,128)(2,1)}, u32[]{:S(2)}) copy-start(bf16[512,256]{1,0:T(8,128)(2,1)} %refs_3_.1) | copy-start | bytes 786436
  3.6 0.9 %copy-start.3 = (bf16[8,32,256]{2,1,0:T(8,128)(2,1)S(1)}, bf16[8,32,256]{2,1,0:T(8,128)(2,1)}, u32[]{:S(2)}) copy-start(bf16[8,32,256]{2,1,0:T(8,128)(2,1)} %refs_0_.3) | copy-start | bytes 393220
  4.5 0.8 %copy-start.5 = (bf16[256,128]{1,0:T(8,128)(2,1)S(1)}, bf16[256,128]{1,0:T(8,128)(2,1)}, u32[]{:S(2)}) copy-start(bf16[256,128]{1,0:T(8,128)(2,1)} %refs_4_.3) | copy-start | bytes 196612
  5.3 18.4 %copy-start.10 = (bf16[256,256]{1,0:T(8,128)(2,1)S(1)}, bf16[256,256]{1,0:T(8,128)(2,1)}, u32[]{:S(2)}) copy-start(bf16[256,256]{1,0:T(8,128)(2,1)} %refs_4_.5) | copy-start | bytes 393220
  5.3 18.4 %copy-start.11 = (bf16[256,256]{1,0:T(8,128)(2,1)S(1)}, bf16[256,256]{1,0:T(8,128)(2,1)}, u32[]{:S(2)}) copy-start(bf16[256,256]{1,0:T(8,128)(2,1)} %refs_5_.3) | copy-start | bytes 393220
  5.3 18.5 %copy-start.12 = (bf16[256,128]{1,0:T(8,128)(2,1)S(1)}, bf16[256,128]{1,0:T(8,128)(2,1)}, u32[]{:S(2)}) copy-start(bf16[256,128]{1,0:T(8,128)(2,1)} %refs_6_.3) | copy-start | bytes 196612
  7.0 21.4 %collective-permute-start.2 = (bf16[384,384]{1,0:T(8,128)(2,1)S(1)}, bf16[384,384]{1,0:T(8,128)(2,1)S(1)}, u32[]{:S(2)}, u32[]{:S(2)}) collective-permute-start(bf16[384,384]{1,0:T(8,128)(2,1)S(1)} %get-tuple-element.18.refs_7_), channel_id=1, source_target_pairs={{4,0},{0,4},{12,8},{8,12},{5,1},{1,5},{13,9},{9,13},{6,2},{2,6},{1... | collective-permute-start | bytes 884744 | tf_op jit(solution)/shard_map/ppermute | solution.py:335
  10.1 7.8 %collective-permute-start.3 = (bf16[144,256]{1,0:T(8,128)(2,1)S(1)}, bf16[144,256]{1,0:T(8,128)(2,1)S(1)}, u32[]{:S(2)}, u32[]{:S(2)}) collective-permute-start(bf16[144,256]{1,0:T(8,128)(2,1)S(1)} %get-tuple-element.17.refs_1_), channel_id=1, source_target_pairs={{8,0},{12,4},{0,8},{4,12},{9,1},{13,5},{1,9},{5,13},{10,2},{14,6},... | collective-permute-start | bytes 221192 | tf_op jit(solution)/shard_map/ppermute | solution.py:223
  17.9 4.4 %collective-permute-start.4 = (bf16[144,256]{1,0:T(8,128)(2,1)S(1)}, bf16[144,256]{1,0:T(8,128)(2,1)S(1)}, u32[]{:S(2)}, u32[]{:S(2)}) collective-permute-start(bf16[144,256]{1,0:T(8,128)(2,1)S(1)} %collective-permute-done.3.refs_0_), channel_id=1, source_target_pairs={{2,0},{0,2},{3,1},{1,3},{6,4},{4,6},{7,5},{5,7},{10,8},{8,10},{11,... | collective-permute-start | bytes 221192 | tf_op jit(solution)/shard_map/ppermute | solution.py:218
  19.4 4.4 %collective-permute-start = (bf16[144,256]{1,0:T(8,128)(2,1)S(1)}, bf16[144,256]{1,0:T(8,128)(2,1)S(1)}, u32[]{:S(2)}, u32[]{:S(2)}) collective-permute-start(bf16[144,256]{1,0:T(8,128)(2,1)S(1)} %get-tuple-element.17.refs_1_), channel_id=1, source_target_pairs={{2,0},{0,2},{3,1},{1,3},{6,4},{4,6},{7,5},{5,7},{10,8},{8,10},{11,... | collective-permute-start | bytes 221192 | tf_op jit(solution)/shard_map/ppermute | solution.py:218
  20.0 3.8 %collective-permute-start.5 = (bf16[144,256]{1,0:T(8,128)(2,1)S(1)}, bf16[144,256]{1,0:T(8,128)(2,1)S(1)}, u32[]{:S(2)}, u32[]{:S(2)}) collective-permute-start(bf16[144,256]{1,0:T(8,128)(2,1)S(1)} %collective-permute-done.3.refs_0_), channel_id=1, source_target_pairs={{1,0},{0,1},{3,2},{2,3},{5,4},{4,5},{7,6},{6,7},{9,8},{8,9},{11,10... | collective-permute-start | bytes 221192 | tf_op jit(solution)/shard_map/ppermute | solution.py:218
  22.3 1.5 %collective-permute-start.6 = (bf16[144,256]{1,0:T(8,128)(2,1)S(1)}, bf16[144,256]{1,0:T(8,128)(2,1)S(1)}, u32[]{:S(2)}, u32[]{:S(2)}) collective-permute-start(bf16[144,256]{1,0:T(8,128)(2,1)S(1)} %collective-permute-done.4.refs_1_), channel_id=1, source_target_pairs={{1,0},{0,1},{3,2},{2,3},{5,4},{4,5},{7,6},{6,7},{9,8},{8,9},{11,10... | collective-permute-start | bytes 221192 | tf_op jit(solution)/shard_map/ppermute | solution.py:218
  23.8 5.5 %collective-permute-start.1 = (bf16[144,256]{1,0:T(8,128)(2,1)S(1)}, bf16[144,256]{1,0:T(8,128)(2,1)S(1)}, u32[]{:S(2)}, u32[]{:S(2)}) collective-permute-start(bf16[144,256]{1,0:T(8,128)(2,1)S(1)} %collective-permute-done.refs_2_), channel_id=1, source_target_pairs={{1,0},{0,1},{3,2},{2,3},{5,4},{4,5},{7,6},{6,7},{9,8},{8,9},{11,10... | collective-permute-start | bytes 221192 | tf_op jit(solution)/shard_map/ppermute | solution.py:218
  25.0 6.4 %collective-permute-start.7 = (bf16[64,384]{1,0:T(8,128)(2,1)S(1)}, bf16[64,384]{1,0:T(8,128)(2,1)S(1)}, u32[]{:S(2)}, u32[]{:S(2)}) collective-permute-start(bf16[64,384]{1,0:T(8,128)(2,1)S(1)} %get-tuple-element.25), channel_id=1, source_target_pairs={{8,0},{12,4},{0,8},{4,12},{9,1},{13,5},{1,9},{5,13},{10,2},{14,6},... | collective-permute-start | bytes 147464 | tf_op jit(solution)/shard_map/ppermute | solution.py:223
  28.4 0.9 %copy-start.4 = (bf16[8,32,256]{2,1,0:T(8,128)(2,1)S(1)}, bf16[8,32,256]{2,1,0:T(8,128)(2,1)}, u32[]{:S(2)}) copy-start(bf16[8,32,256]{2,1,0:T(8,128)(2,1)} %refs_0_.3) | copy-start | bytes 393220
  29.3 5.8 %collective-permute-start.8 = (bf16[64,384]{1,0:T(8,128)(2,1)S(1)}, bf16[64,384]{1,0:T(8,128)(2,1)S(1)}, u32[]{:S(2)}, u32[]{:S(2)}) collective-permute-start(bf16[64,384]{1,0:T(8,128)(2,1)S(1)} %shard_map.122), channel_id=1, source_target_pairs={{8,0},{12,4},{0,8},{4,12},{9,1},{13,5},{1,9},{5,13},{10,2},{14,6},... | collective-permute-start | bytes 147464 | tf_op jit(solution)/shard_map/ppermute | solution.py:223

commit v4 on v3

--- a/solution.py
+++ b/solution.py
@@ -20,13 +20,10 @@
 HBM = pl.BlockSpec(memory_space=pltpu.HBM)
 
 
-def near(array):
-    return pltpu.with_memory_space_constraint(array, pltpu.VMEM)
-
-
 def call(kernel, out_shape, in_specs, out_specs, args, flops, scratch=()):
     moved = sum(math.prod(a.shape) * a.dtype.itemsize for a in args)
-    args = [near(a) if spec is VMEM else a for a, spec in zip(args, in_specs)]
+    spaces = {id(VMEM): pltpu.VMEM, id(HBM): pltpu.HBM}
+    args = [pltpu.with_memory_space_constraint(a, spaces[id(spec)]) for a, spec in zip(args, in_specs)]
     return pl.pallas_call(
         kernel,
         out_shape=out_shape,
@@ -38,52 +35,52 @@
     )(*args)
 
 
-def prepare_kernel(shares, *refs):
-    sources, outs, scratch = refs[:9], refs[9:13], refs[13:]
-    history_ref, sources = sources[0], sources[1:]
-    piece_ref, items_out, heads_ref, bias_out = outs
-    held, sems, token_sem = scratch[:8], scratch[8], scratch[9]
-    copies = [pltpu.make_async_copy(*pair, sems.at[i]) for i, pair in enumerate(zip(sources, held))]
+def fetch_kernel(shares, *refs):
+    history_ref, sources = refs[0], refs[1:9]
+    piece_ref, heads_ref, bias_out, *fetched = refs[9:17]
+    w_task_ref, bias_ref, lengths_ref, sems = refs[17:]
     users, tokens, _ = history_ref.shape
     users //= shares
+    width = piece_ref.shape[1]
     first = lax.axis_index("sub") * users
-    width = piece_ref.shape[1]
-    moves = []
+    pairs = []
     for user in range(users):
         place = piece_ref.at[pl.ds(user * tokens, tokens)]
-        moves.append(pltpu.make_async_copy(history_ref.at[first + user], place, token_sem.at[user]))
-    for copy in copies + moves:
+        pairs.append((history_ref.at[first + user], place))
+    pairs += zip(sources, (lengths_ref, w_task_ref, bias_ref, *fetched))
+    copies = [pltpu.make_async_copy(*pair, sems.at[i]) for i, pair in enumerate(pairs)]
+    for copy in copies:
         copy.start()
-    rows_ref, w_query_ref, w_item_ref, w_joint_ref, bias_ref, w_task_ref, bias_task_ref, lengths_ref = held
-
-    for copy in copies[5:]:
-        copy.wait()
+    copies[users].wait()
     row = lax.broadcasted_iota(jnp.int32, (LENGTH_ROWS, width), 0)
     lengths = jnp.zeros((LENGTH_ROWS, width), F32)
     for user in range(users):
         lengths = jnp.where(row == user, lengths_ref[first + user].astype(F32), lengths)
     piece_ref[users * tokens :, :] = lengths.astype(BF16)
+    copies[users + 1].wait()
     tasks, hid = w_task_ref.shape
     w_task = w_task_ref[...].astype(F32)
     blank = jnp.zeros_like(w_task)
     heads_ref[:, :hid] = jnp.concatenate([w_task, blank], 0).astype(BF16)
     heads_ref[:, hid:] = jnp.concatenate([blank, w_task], 0).astype(BF16)
+    copies[users + 2].wait()
     row = lax.broadcasted_iota(jnp.int32, bias_out.shape, 0) % tasks
     bias = jnp.zeros(bias_out.shape, F32)
     for task in range(tasks):
-        bias = jnp.where(row == task, bias_task_ref[task], bias)
+        bias = jnp.where(row == task, bias_ref[task], bias)
     bias_out[...] = bias
-
-    for copy in copies[:5]:
+    for copy in copies[:users] + copies[users + 3 :]:
         copy.wait()
-    rows = rows_ref[...]
+
+
+def project_kernel(items_ref, w_query_ref, w_item_ref, w_joint_ref, bias_ref, out_ref):
+    width = w_query_ref.shape[1]
+    rows = items_ref[...]
     queries = jnp.dot(rows, w_query_ref[...], preferred_element_type=F32)
-    items_out[:width, :] = queries.T.astype(BF16)
+    out_ref[:width, :] = queries.T.astype(BF16)
     joined = jnp.dot(rows, w_item_ref[...], preferred_element_type=F32).astype(BF16)
     terms = jnp.dot(joined, w_joint_ref[...], preferred_element_type=F32) + bias_ref[...]
-    items_out[width:, :] = terms.T.astype(BF16)
-    for move in moves:
-        move.wait()
+    out_ref[width:, :] = terms.T.astype(BF16)
 
 
 def keys_values(pieces, turn, w_key_ref, w_value_ref, w_pooled_ref, key_ref, pooled_ref, mask_ref, history_ref):
@@ -258,26 +255,34 @@
     count, parts, shares = (lax.axis_size(axis) for axis in ("blk", "users", "sub"))
     full = tokens * parts
 
-    sources = (item_rows, w_query, w_item, w_joint, bias_hidden[None], w_task.T)
-    piece, mine, heads, bias = call(
-        functools.partial(prepare_kernel, shares),
+    share = users // shares
+    operands = (item_rows, w_query, w_item, w_joint, bias_hidden[None])
+    piece, heads, bias, *fetched = call(
+        functools.partial(fetch_kernel, shares),
         (
-            pltpu.VMEM((users // shares * tokens + LENGTH_ROWS, width), BF16),
-            pltpu.VMEM((width + hid, items), BF16),
+            pltpu.VMEM((share * tokens + LENGTH_ROWS, width), BF16),
             pltpu.VMEM((2 * tasks, 2 * hid), BF16),
             pltpu.VMEM((2 * tasks, 128), F32),
+            *(pltpu.VMEM(a.shape, a.dtype) for a in operands),
         ),
         [HBM] * 9,
-        [VMEM] * 4,
-        (history, *sources, bias_task, lengths),
-        2 * items * item_rows.shape[1] * 2 * width,
+        [VMEM] * 8,
+        (history, lengths, w_task.T, bias_task, *operands),
+        0,
         (
-            *(pltpu.VMEM(a.shape, a.dtype) for a in sources),
+            pltpu.VMEM((tasks, hid), BF16),
             pltpu.SMEM(bias_task.shape, F32),
             pltpu.SMEM(lengths.shape, jnp.int32),
-            pltpu.SemaphoreType.DMA((8,)),
-            pltpu.SemaphoreType.DMA((users // shares,)),
+            pltpu.SemaphoreType.DMA((share + 8,)),
         ),
+    )
+    mine = call(
+        project_kernel,
+        pltpu.VMEM((width + hid, items), BF16),
+        [VMEM] * 5,
+        VMEM,
+        fetched,
+        2 * items * item_rows.shape[1] * 2 * width,
     )
     flops = 2 * users * items * (full * (width + hid) + hid * tasks)
     state = (

time: 36.4 us -> 31.3 us (0.86)
  local copies, waits for them, and re-layouts: 5.35 us -> 0.02 us
    unnamed x26 -> x8, local copies, waits for them, and re-layouts: 5.35 us -> 0.02 us
    pallas_call x6 -> x7, Pallas kernels: 6.73 us -> 7.08 us  [call(): pl.pallas_call(kernel, out_shape=out_shape, in_specs=in_specs, out_specs=...]
  transfers between devices with their start and end apart: 9 -> 9, of which waited for: 4 -> 4; matrix products, arithmetic and copies ran while one was open for 0% -> 0% of each run, Pallas kernels for 11% -> 13%
where the time goes in v4:
time: 31.3 us; the launch traced here: 31.2 us
  waiting for transfers between devices  12.8 us (41%)
  starting transfers between devices  11.2 us (36%)
  Pallas kernels  7.08 us (23%)
    ppermute x3, waiting for transfers between devices, from_pair(): lax.ppermute(block, 'blk', [((i + 2 * distance) % count, i) for i in rang...  8.98 us
    pallas_call x7, Pallas kernels, call(): pl.pallas_call(kernel, out_shape=out_shape, in_specs=in_specs, out_specs=...  7.08 us
    ppermute x3, starting transfers between devices, from_pair(): lax.ppermute(block, 'blk', [((i + 2 * distance) % count, i) for i in rang...  6.01 us
    ppermute x5, waiting for transfers between devices, shift(): lax.ppermute(block, axis, [((i + distance) % count, i) for i in range(cou...  3.82 us
    ppermute x1, starting transfers between devices, shards(): other = lax.ppermute(mine, 'blk', [(i ^ 1, i) for i in range(count)])  3.12 us
    ppermute x5, starting transfers between devices, shift(): lax.ppermute(block, axis, [((i + distance) % count, i) for i in range(cou...  2.03 us
  transfers between devices with their start and end apart: 9, of which 4 were waited for; matrix products, arithmetic and copies ran while one was open for 0% of the time, Pallas kernels for 13%

profile of v4, /device:TPU:0, one launch (start us, length us, event | category | flops | bytes accessed | tf_op | source)
XLA Modules:
  0.0 31.2 jit_solution(8813310308426554449)
XLA Ops:
  0.0 1.3 %shard_map.118 = (bf16[144,256]{1,0:T(8,128)(2,1)S(1)}, bf16[16,256]{1,0:T(8,128)(2,1)S(1)}, f32[16,128]{1,0:T(8,128)S(1)}, bf16[384,512]{1,0:T(8,128)(2,1)S(1)}...) custom-call(bf16[8,32,256]{2,1,0:T(8,128)(2,1)} %refs_0_.3, ...), custom_call_target="tpu_custom_call" | custom-call | bytes 1116736 | tf_op jit(solution)/shard_map/pallas_call | solution.py:27
  1.3 0.0 copy-start.1
  1.4 0.0 copy-start.2
  1.4 0.0 copy-start.3
  1.4 0.6 %shard_map.119.refs_7_ = bf16[384,384]{1,0:T(8,128)(2,1)S(1)} custom-call(bf16[384,512]{1,0:T(8,128)(2,1)S(1)} %get-tuple-element.22.items_ref, bf16[512,256]{1,0:T(8,128)(2,1)S(1)} %get-tuple-element.23.w_query_ref, bf16[512,256]{1,0:T(8,128)(2,1)S(1)} %get-tuple-element.24.w_item_ref, bf16[256,128]{1,0:T(8,128)(2,1)S(1)} %get-tuple-element.25.w_joint_ref, ...), custom_call_target="tpu_custom_call" | custom-call | flops 201326592 | bytes 983552 | tf_op jit(solution)/shard_map/pallas_call | solution.py:27
  2.0 3.1 %collective-permute-start.2 = (bf16[384,384]{1,0:T(8,128)(2,1)S(1)}, bf16[384,384]{1,0:T(8,128)(2,1)S(1)}, u32[]{:S(2)}, u32[]{:S(2)}) collective-permute-start(bf16[384,384]{1,0:T(8,128)(2,1)S(1)} %shard_map.119.refs_7_), channel_id=1, source_target_pairs={{4,0},{0,4},{12,8},{8,12},{5,1},{1,5},{13,9},{9,13},{6,2},{2,6},{1... | collective-permute-start | bytes 884744 | tf_op jit(solution)/shard_map/ppermute | solution.py:340
  5.1 2.6 %collective-permute-start.3 = (bf16[144,256]{1,0:T(8,128)(2,1)S(1)}, bf16[144,256]{1,0:T(8,128)(2,1)S(1)}, u32[]{:S(2)}, u32[]{:S(2)}) collective-permute-start(bf16[144,256]{1,0:T(8,128)(2,1)S(1)} %get-tuple-element.21.refs_1_), channel_id=1, source_target_pairs={{8,0},{12,4},{0,8},{4,12},{9,1},{13,5},{1,9},{5,13},{10,2},{14,6},... | collective-permute-start | bytes 221192 | tf_op jit(solution)/shard_map/ppermute | solution.py:220
  7.7 5.3 %collective-permute-done.3.refs_0_ = bf16[144,256]{1,0:T(8,128)(2,1)S(1)} collective-permute-done((bf16[144,256]{1,0:T(8,128)(2,1)S(1)}, bf16[144,256]{1,0:T(8,128)(2,1)S(1)}, u32[]{:S(2)}, u32[]{:S(2)}) %collective-permute-start.3) | collective-permute-done | bytes 73760 | tf_op jit(solution)/shard_map/ppermute | solution.py:220
  13.0 1.5 %collective-permute-start.4 = (bf16[144,256]{1,0:T(8,128)(2,1)S(1)}, bf16[144,256]{1,0:T(8,128)(2,1)S(1)}, u32[]{:S(2)}, u32[]{:S(2)}) collective-permute-start(bf16[144,256]{1,0:T(8,128)(2,1)S(1)} %collective-permute-done.3.refs_0_), channel_id=1, source_target_pairs={{2,0},{0,2},{3,1},{1,3},{6,4},{4,6},{7,5},{5,7},{10,8},{8,10},{11,... | collective-permute-start | bytes 221192 | tf_op jit(solution)/shard_map/ppermute | solution.py:215
  14.5 0.5 %collective-permute-start = (bf16[144,256]{1,0:T(8,128)(2,1)S(1)}, bf16[144,256]{1,0:T(8,128)(2,1)S(1)}, u32[]{:S(2)}, u32[]{:S(2)}) collective-permute-start(bf16[144,256]{1,0:T(8,128)(2,1)S(1)} %get-tuple-element.21.refs_1_), channel_id=1, source_target_pairs={{2,0},{0,2},{3,1},{1,3},{6,4},{4,6},{7,5},{5,7},{10,8},{8,10},{11,... | collective-permute-start | bytes 221192 | tf_op jit(solution)/shard_map/ppermute | solution.py:215
  15.0 0.0 collective-permute-start.5
  15.0 2.3 %collective-permute-done.4.refs_1_ = bf16[144,256]{1,0:T(8,128)(2,1)S(1)} collective-permute-done((bf16[144,256]{1,0:T(8,128)(2,1)S(1)}, bf16[144,256]{1,0:T(8,128)(2,1)S(1)}, u32[]{:S(2)}, u32[]{:S(2)}) %collective-permute-start.4) | collective-permute-done | bytes 73760 | tf_op jit(solution)/shard_map/ppermute | solution.py:215
  17.3 0.0 collective-permute-start.6
  17.3 1.5 %collective-permute-done.refs_2_ = bf16[144,256]{1,0:T(8,128)(2,1)S(1)} collective-permute-done((bf16[144,256]{1,0:T(8,128)(2,1)S(1)}, bf16[144,256]{1,0:T(8,128)(2,1)S(1)}, u32[]{:S(2)}, u32[]{:S(2)}) %collective-permute-start) | collective-permute-done | bytes 73760 | tf_op jit(solution)/shard_map/ppermute | solution.py:215
  18.8 0.0 collective-permute-start.1
  18.8 0.0 collective-permute-done.5.refs_2_
  18.8 0.0 collective-permute-done.6.refs_3_
  18.8 0.0 copy-done.1
  18.8 0.0 copy-done.2
  18.8 0.0 copy-done.3
  18.9 1.2 %shard_map.122 = (bf16[64,384]{1,0:T(8,128)(2,1)S(1)}, bf16[512,256]{1,0:T(8,128)(2,1)S(1)}, bf16[4,256,256]{2,1,0:T(8,128)(2,1)S(1)}, f32[512,128]{1,0:T(8,128)S(1)}) custom-call(bf16[144,256]{1,0:T(8,128)(2,1)S(1)} %collective-permute-done.3.refs_0_, bf16[144,256]{1,0:T(8,128)(2,1)S(1)} %collective-permute-done.4.refs_1_, ...), custom_call_target="tpu_custom_call" | custom-call | flops 291504128 | bytes 933888 | tf_op jit(solution)/shard_map/pallas_call | solution.py:27
  20.1 3.4 %collective-permute-start.7 = (bf16[64,384]{1,0:T(8,128)(2,1)S(1)}, bf16[64,384]{1,0:T(8,128)(2,1)S(1)}, u32[]{:S(2)}, u32[]{:S(2)}) collective-permute-start(bf16[64,384]{1,0:T(8,128)(2,1)S(1)} %get-tuple-element.33), channel_id=1, source_target_pairs={{8,0},{12,4},{0,8},{4,12},{9,1},{13,5},{1,9},{5,13},{10,2},{14,6},... | collective-permute-start | bytes 147464 | tf_op jit(solution)/shard_map/ppermute | solution.py:220
  23.4 0.0 collective-permute-done.2.items_ref
  23.4 0.0 copy-start
  23.4 0.9 %shard_map.123 = bf16[64,384]{1,0:T(8,128)(2,1)S(1)} custom-call(bf16[384,384]{1,0:T(8,128)(2,1)S(1)} %collective-permute-done.2.items_ref, bf16[512,256]{1,0:T(8,128)(2,1)S(1)} %get-tuple-element.34.key_ref, bf16[4,256,256]{2,1,0:T(8,128)(2,1)S(1)} %get-tuple-element.35.pooled_ref, f32[512,128]{1,0:T(8,128)S(1)} %get-tuple-element.36.mask_ref, ...), custom_call_target="tpu_custom_call" | custom-call | flops 157286400 | bytes 1359872 | tf_op jit(solution)/shard_map/pallas_call | solution.py:27
  24.3 0.0 collective-permute-start.8
  24.3 0.0 collective-permute-done.1.refs_3_
  24.4 0.0 copy-done
  24.4 1.2 %shard_map.120 = (f32[8,8,384]{2,1,0:T(8,128)S(1)}, bf16[512,256]{1,0:T(8,128)(2,1)S(1)}, bf16[4,256,256]{2,1,0:T(8,128)(2,1)S(1)}, f32[512,128]{1,0:T(8,128)S(1)}) custom-call(bf16[8,32,256]{2,1,0:T(8,128)(2,1)S(1)} %copy-done, bf16[144,256]{1,0:T(8,128)(2,1)S(1)} %get-tuple-element.21.refs_1_, bf16[144,256]{1,0:T(8,128)(2,1)S(1)} %collective-permute-done.refs_2_, ...), custom_call_target="tpu_custom_call" | custom-call | flops 291504128 | bytes 991232 | tf_op jit(solution)/shard_map/pallas_call | solution.py:27
  25.6 0.9 %shard_map.121.refs_1_ = f32[8,8,384]{2,1,0:T(8,128)S(1)} custom-call(bf16[384,384]{1,0:T(8,128)(2,1)S(1)} %collective-permute-done.2.items_ref, bf16[512,256]{1,0:T(8,128)(2,1)S(1)} %get-tuple-element.30.key_ref, bf16[4,256,256]{2,1,0:T(8,128)(2,1)S(1)} %get-tuple-element.31.pooled_ref, f32[512,128]{1,0:T(8,128)S(1)} %get-tuple-element.32.mask_ref, ...), custom_call_target="tpu_custom_call" | custom-call | flops 157286400 | bytes 1359872 | tf_op jit(solution)/shard_map/pallas_call | solution.py:27
  26.4 0.0 collective-permute-done.7.refs_2_
  26.4 3.7 %collective-permute-done.8.refs_3_ = bf16[64,384]{1,0:T(8,128)(2,1)S(1)} collective-permute-done((bf16[64,384]{1,0:T(8,128)(2,1)S(1)}, bf16[64,384]{1,0:T(8,128)(2,1)S(1)}, u32[]{:S(2)}, u32[]{:S(2)}) %collective-permute-start.8) | collective-permute-done | bytes 49184 | tf_op jit(solution)/shard_map/ppermute | solution.py:220
  30.2 1.0 %shard_map.124 = f32[8,9,8,384]{3,2,1,0:T(8,128)} custom-call(f32[8,8,384]{2,1,0:T(8,128)S(1)} %get-tuple-element.29.refs_0_, f32[8,8,384]{2,1,0:T(8,128)S(1)} %shard_map.121.refs_1_, bf16[64,384]{1,0:T(8,128)(2,1)S(1)} %collective-permute-done.7.refs_2_, bf16[64,384]{1,0:T(8,128)(2,1)S(1)} %collective-permute-done.8.refs_3_), custom_call_target="tpu_custom_call" | custom-call | bytes 294912 | tf_op jit(solution)/shard_map/pallas_call | solution.py:27
Async XLA Ops:
  1.3 17.5 %copy-start.1 = (bf16[256,256]{1,0:T(8,128)(2,1)S(1)}, bf16[256,256]{1,0:T(8,128)(2,1)}, u32[]{:S(2)}) copy-start(bf16[256,256]{1,0:T(8,128)(2,1)} %refs_4_.5) | copy-start | bytes 393220
  1.4 17.5 %copy-start.2 = (bf16[256,256]{1,0:T(8,128)(2,1)S(1)}, bf16[256,256]{1,0:T(8,128)(2,1)}, u32[]{:S(2)}) copy-start(bf16[256,256]{1,0:T(8,128)(2,1)} %refs_5_.5) | copy-start | bytes 393220
  1.4 17.5 %copy-start.3 = (bf16[256,128]{1,0:T(8,128)(2,1)S(1)}, bf16[256,128]{1,0:T(8,128)(2,1)}, u32[]{:S(2)}) copy-start(bf16[256,128]{1,0:T(8,128)(2,1)} %refs_6_.5) | copy-start | bytes 196612
  2.0 21.4 %collective-permute-start.2 = (bf16[384,384]{1,0:T(8,128)(2,1)S(1)}, bf16[384,384]{1,0:T(8,128)(2,1)S(1)}, u32[]{:S(2)}, u32[]{:S(2)}) collective-permute-start(bf16[384,384]{1,0:T(8,128)(2,1)S(1)} %shard_map.119.refs_7_), channel_id=1, source_target_pairs={{4,0},{0,4},{12,8},{8,12},{5,1},{1,5},{13,9},{9,13},{6,2},{2,6},{1... | collective-permute-start | bytes 884744 | tf_op jit(solution)/shard_map/ppermute | solution.py:340
  5.1 7.8 %collective-permute-start.3 = (bf16[144,256]{1,0:T(8,128)(2,1)S(1)}, bf16[144,256]{1,0:T(8,128)(2,1)S(1)}, u32[]{:S(2)}, u32[]{:S(2)}) collective-permute-start(bf16[144,256]{1,0:T(8,128)(2,1)S(1)} %get-tuple-element.21.refs_1_), channel_id=1, source_target_pairs={{8,0},{12,4},{0,8},{4,12},{9,1},{13,5},{1,9},{5,13},{10,2},{14,6},... | collective-permute-start | bytes 221192 | tf_op jit(solution)/shard_map/ppermute | solution.py:220
  13.0 4.4 %collective-permute-start.4 = (bf16[144,256]{1,0:T(8,128)(2,1)S(1)}, bf16[144,256]{1,0:T(8,128)(2,1)S(1)}, u32[]{:S(2)}, u32[]{:S(2)}) collective-permute-start(bf16[144,256]{1,0:T(8,128)(2,1)S(1)} %collective-permute-done.3.refs_0_), channel_id=1, source_target_pairs={{2,0},{0,2},{3,1},{1,3},{6,4},{4,6},{7,5},{5,7},{10,8},{8,10},{11,... | collective-permute-start | bytes 221192 | tf_op jit(solution)/shard_map/ppermute | solution.py:215
  14.5 4.4 %collective-permute-start = (bf16[144,256]{1,0:T(8,128)(2,1)S(1)}, bf16[144,256]{1,0:T(8,128)(2,1)S(1)}, u32[]{:S(2)}, u32[]{:S(2)}) collective-permute-start(bf16[144,256]{1,0:T(8,128)(2,1)S(1)} %get-tuple-element.21.refs_1_), channel_id=1, source_target_pairs={{2,0},{0,2},{3,1},{1,3},{6,4},{4,6},{7,5},{5,7},{10,8},{8,10},{11,... | collective-permute-start | bytes 221192 | tf_op jit(solution)/shard_map/ppermute | solution.py:215
  15.0 3.8 %collective-permute-start.5 = (bf16[144,256]{1,0:T(8,128)(2,1)S(1)}, bf16[144,256]{1,0:T(8,128)(2,1)S(1)}, u32[]{:S(2)}, u32[]{:S(2)}) collective-permute-start(bf16[144,256]{1,0:T(8,128)(2,1)S(1)} %collective-permute-done.3.refs_0_), channel_id=1, source_target_pairs={{1,0},{0,1},{3,2},{2,3},{5,4},{4,5},{7,6},{6,7},{9,8},{8,9},{11,10... | collective-permute-start | bytes 221192 | tf_op jit(solution)/shard_map/ppermute | solution.py:215
  17.3 1.5 %collective-permute-start.6 = (bf16[144,256]{1,0:T(8,128)(2,1)S(1)}, bf16[144,256]{1,0:T(8,128)(2,1)S(1)}, u32[]{:S(2)}, u32[]{:S(2)}) collective-permute-start(bf16[144,256]{1,0:T(8,128)(2,1)S(1)} %collective-permute-done.4.refs_1_), channel_id=1, source_target_pairs={{1,0},{0,1},{3,2},{2,3},{5,4},{4,5},{7,6},{6,7},{9,8},{8,9},{11,10... | collective-permute-start | bytes 221192 | tf_op jit(solution)/shard_map/ppermute | solution.py:215
  18.8 5.5 %collective-permute-start.1 = (bf16[144,256]{1,0:T(8,128)(2,1)S(1)}, bf16[144,256]{1,0:T(8,128)(2,1)S(1)}, u32[]{:S(2)}, u32[]{:S(2)}) collective-permute-start(bf16[144,256]{1,0:T(8,128)(2,1)S(1)} %collective-permute-done.refs_2_), channel_id=1, source_target_pairs={{1,0},{0,1},{3,2},{2,3},{5,4},{4,5},{7,6},{6,7},{9,8},{8,9},{11,10... | collective-permute-start | bytes 221192 | tf_op jit(solution)/shard_map/ppermute | solution.py:215
  20.1 6.4 %collective-permute-start.7 = (bf16[64,384]{1,0:T(8,128)(2,1)S(1)}, bf16[64,384]{1,0:T(8,128)(2,1)S(1)}, u32[]{:S(2)}, u32[]{:S(2)}) collective-permute-start(bf16[64,384]{1,0:T(8,128)(2,1)S(1)} %get-tuple-element.33), channel_id=1, source_target_pairs={{8,0},{12,4},{0,8},{4,12},{9,1},{13,5},{1,9},{5,13},{10,2},{14,6},... | collective-permute-start | bytes 147464 | tf_op jit(solution)/shard_map/ppermute | solution.py:220
  23.4 0.9 %copy-start = (bf16[8,32,256]{2,1,0:T(8,128)(2,1)S(1)}, bf16[8,32,256]{2,1,0:T(8,128)(2,1)}, u32[]{:S(2)}) copy-start(bf16[8,32,256]{2,1,0:T(8,128)(2,1)} %refs_0_.3) | copy-start | bytes 393220
  24.3 5.8 %collective-permute-start.8 = (bf16[64,384]{1,0:T(8,128)(2,1)S(1)}, bf16[64,384]{1,0:T(8,128)(2,1)S(1)}, u32[]{:S(2)}, u32[]{:S(2)}) collective-permute-start(bf16[64,384]{1,0:T(8,128)(2,1)S(1)} %shard_map.123), channel_id=1, source_target_pairs={{8,0},{12,4},{0,8},{4,12},{9,1},{13,5},{1,9},{5,13},{10,2},{14,6},... | collective-permute-start | bytes 147464 | tf_op jit(solution)/shard_map/ppermute | solution.py:220
